TPU v7x, 32 devices: a whole 2x2x4 slice. The times are simulated.
32 devices in a mesh: dp: 8 (over y, x, core), seq: 4 (over z).
Axes of the slice: x: 2, y: 2, z: 4, core: 2. Of those that a mesh axis runs over, the one named last changes fastest.
Arguments:
- enc_states: bfloat16 [8, 256, 4096], P('dp'), may hold values from -6 to 6
- lengths: int32 [8], replicated, may hold values from 1 to 128, as said below
- prompt_owner_sample: int32 [8], replicated, may hold values from 0 to 7, each once
- t5_gain: float32 [4096], replicated, may hold values from 0.5 to 1.5
- t5_in_weight: bfloat16 [2, 4096, 5120], P(None, None, 'seq'), may hold values from -0.09375 to 0.09375
- t5_out_weight: bfloat16 [5120, 4096], P('seq'), may hold values from -0.078125 to 0.078125
- t5_final_gain: float32 [4096], replicated, may hold values from 0.5 to 1.5
- context_weight: bfloat16 [4096, 3072], P('seq', 'dp'), may hold values from -0.09375 to 0.09375
- text_shift: float32 [8, 3072], P('dp'), may hold values from -3 to 3
- text_scale: float32 [8, 3072], P('dp'), may hold values from -0.5 to 0.5
- kv_weight: bfloat16 [3072, 2, 3072], P('dp', None, 'seq'), may hold values from -0.109375 to 0.109375
- text_key_gain: float32 [128], replicated, may hold values from 0.25 to 1.75
- image_query_key_value: bfloat16 [8, 512, 3, 3072], P('dp', 'seq'), may hold values from -6 to 6
- image_qk_gain: float32 [2, 128], replicated, may hold values from 0.25 to 1.75
- proj_weight: bfloat16 [3072, 3072], P('seq', 'dp'), may hold values from -0.109375 to 0.109375
- dora_a: float32 [3072, 64], P('seq'), may hold values from -0.109375 to 0.109375
- dora_b: float32 [64, 3072], P(None, 'dp'), may hold values from -0.375 to 0.375
- magnitude: float32 [3072], P('dp'), may hold values from 0.5 to 2
- grad_out: bfloat16 [8, 512, 3072], P('dp', 'seq'), may hold values from -6 to 6
Outputs:
- image_out: bfloat16 [8, 512, 3072], P('dp', 'seq')
- grad_a: float32 [3072, 64], P('seq')
- grad_b: float32 [64, 3072], P(None, 'dp')
- grad_magnitude: float32 [3072], P('dp')
Inputs may be any that keep to these rules, and one draw needn't show every extreme that they name: `lengths`: prompt token counts; in every draw one prompt has exactly 128 tokens. `prompt_owner_sample`: each DiT sample index appears exactly once.
All inputs are finite; a program needn't handle non-finite values.
Results may differ from a plain program's by a relative error of at most 0.024.
Values may be sent and summed in bfloat16 or wider, within the bound.
A program may use at most 128 MiB of HBM per device.

v0:
```python
import math

import jax
import jax.numpy as jnp
from jax import lax
from jax.sharding import PartitionSpec as P

HD = 128


EPSILON = 1e-06


def rms_scale(values, gain):
    return values * lax.rsqrt(jnp.mean(values * values, -1, keepdims=True) + EPSILON) * gain


def on_device(
    enc_states,
    lengths,
    prompt_owner_sample,
    t5_gain,
    t5_in_weight,
    t5_out_weight,
    t5_final_gain,
    context_weight,
    text_shift,
    text_scale,
    kv_weight,
    text_key_gain,
    image_query_key_value,
    image_qk_gain,
    proj_weight,
    dora_a,
    dora_b,
    magnitude,
    grad_out,
):
    seq_rank = lax.axis_index("seq")
    data_rank = lax.axis_index("dp")
    seq_devices = lax.axis_size("seq")
    tokens = enc_states[0]
    text_length, width_enc = tokens.shape
    feat_width = width_enc // seq_devices
    own_tokens = lax.dynamic_slice_in_dim(tokens, seq_rank * feat_width, feat_width, 1).astype(
        jnp.float32
    )
    own_final = lax.dynamic_slice_in_dim(t5_final_gain, seq_rank * feat_width, feat_width, 0)
    prompt_indices = jnp.arange(prompt_owner_sample.shape[0], dtype=jnp.int32)
    normed = rms_scale(tokens.astype(jnp.float32), t5_gain).astype(jnp.bfloat16)
    gate_proj = jnp.dot(normed, t5_in_weight[0], preferred_element_type=jnp.float32)
    upward = jnp.dot(normed, t5_in_weight[1], preferred_element_type=jnp.float32)
    hidden = (jax.nn.gelu(gate_proj, approximate=True) * upward).astype(jnp.bfloat16)
    ffn_part = lax.psum_scatter(
        jnp.dot(hidden, t5_out_weight, preferred_element_type=jnp.float32).astype(jnp.bfloat16),
        "seq",
        scatter_dimension=1,
        tiled=True,
    ).astype(jnp.float32)
    encoded = ((own_tokens + ffn_part) * own_final).astype(jnp.bfloat16)
    context_part = jnp.dot(
        encoded,
        lax.all_gather(context_weight, "dp", axis=1, tiled=True),
        preferred_element_type=jnp.float32,
    )
    text_tokens = lax.psum_scatter(
        context_part.astype(jnp.bfloat16), "seq", scatter_dimension=0, tiled=True
    )
    source_sample = jnp.sum(jnp.where(prompt_owner_sample == data_rank, prompt_indices, 0))
    diffusion_length = jnp.sum(jnp.where(prompt_indices == source_sample, lengths, 0))
    shard_piece = lax.all_gather(text_tokens[None], "dp", axis=0, tiled=True)
    chosen = jnp.arange(shard_piece.shape[0], dtype=jnp.int32) == source_sample
    picked = jnp.sum(
        jnp.where(chosen[:, None, None], shard_piece, jnp.zeros_like(shard_piece)), 0, keepdims=True
    )
    routed = picked[0]
    routed_values = routed.astype(jnp.float32)
    centre = jnp.mean(routed_values, -1, keepdims=True)
    spread = jnp.mean((routed_values - centre) * (routed_values - centre), -1, keepdims=True)
    layer_normed = (routed_values - centre) * lax.rsqrt(spread + EPSILON)
    modulated = ((1.0 + text_scale) * layer_normed + text_shift).astype(jnp.bfloat16)
    text_all = lax.all_gather(modulated, "seq", axis=0, tiled=True)
    head_width = kv_weight.shape[2]
    local_heads = head_width // HD
    shard_piece = lax.all_gather(kv_weight, "dp", axis=0, tiled=True)
    key_value = jnp.dot(
        text_all,
        shard_piece.reshape(shard_piece.shape[0], 2 * head_width),
        preferred_element_type=jnp.float32,
    )
    key_value = key_value.reshape(text_length, 2, local_heads, HD)
    prompt_key_rows = rms_scale(key_value[:, 0], text_key_gain).astype(jnp.bfloat16)
    prompt_value_rows = key_value[:, 1].astype(jnp.bfloat16)
    exchanged = lax.all_to_all(
        image_query_key_value[0], "seq", split_axis=2, concat_axis=0, tiled=True
    )
    image_len = exchanged.shape[0]
    split_heads = exchanged.reshape(image_len, 3, local_heads, HD)
    queries = rms_scale(split_heads[:, 0].astype(jnp.float32), image_qk_gain[0]).astype(
        jnp.bfloat16
    )
    key_image = rms_scale(split_heads[:, 1].astype(jnp.float32), image_qk_gain[1]).astype(
        jnp.bfloat16
    )
    value_image = split_heads[:, 2]
    key_valid_mask = jnp.arange(text_length, dtype=jnp.int32) < diffusion_length
    score_scale = 1.0 / math.sqrt(HD)
    query_rows = min(512, image_len)
    block_count = image_len // query_rows

    def attend_block(query_block):
        text_scores = (
            jnp.einsum(
                "qhd,khd->hqk", query_block, prompt_key_rows, preferred_element_type=jnp.float32
            )
            * score_scale
        )
        text_weight = jnp.where(key_valid_mask[None, None, :], jnp.exp(text_scores), 0.0)
        image_scores = (
            jnp.einsum("qhd,khd->hqk", query_block, key_image, preferred_element_type=jnp.float32)
            * score_scale
        )
        image_weight = jnp.exp(image_scores)
        denominator = jnp.sum(text_weight, -1) + jnp.sum(image_weight, -1)
        text_probs = (text_weight / denominator[..., None]).astype(jnp.bfloat16)
        image_probs = (image_weight / denominator[..., None]).astype(jnp.bfloat16)
        mixture = jnp.einsum(
            "hqk,khd->qhd", text_probs, prompt_value_rows, preferred_element_type=jnp.float32
        )
        mixture = mixture + jnp.einsum(
            "hqk,khd->qhd", image_probs, value_image, preferred_element_type=jnp.float32
        )
        return mixture.astype(jnp.bfloat16)

    attended_rows = lax.map(
        attend_block, queries.reshape(block_count, query_rows, local_heads, HD)
    ).reshape(image_len, head_width)
    base_rows = lax.all_gather(proj_weight, "dp", axis=1, tiled=True)
    adapter_up, magnitudes = (
        lax.all_gather(dora_b.astype(jnp.bfloat16), "dp", axis=1, tiled=True).astype(dora_b.dtype),
        lax.all_gather(magnitude.astype(jnp.bfloat16), "dp", axis=0, tiled=True).astype(
            magnitude.dtype
        ),
    )
    direction = base_rows.astype(jnp.float32) + jnp.dot(
        dora_a, adapter_up, precision=lax.Precision.HIGHEST
    )
    column_sq = lax.psum(jnp.sum(direction * direction, 0), "seq")
    column_norm = jnp.sqrt(column_sq + EPSILON)
    column_ratio = magnitudes / column_norm
    scaled = (direction * column_ratio).astype(jnp.bfloat16)
    row_block = attended_rows
    image_out = lax.psum_scatter(
        jnp.dot(row_block, scaled, preferred_element_type=jnp.float32).astype(jnp.bfloat16),
        "seq",
        scatter_dimension=0,
        tiled=True,
    )[None]
    row_block = attended_rows
    weight_grad = jnp.einsum(
        "th,td->hd",
        row_block,
        lax.all_gather(grad_out[0], "seq", axis=0, tiled=True),
        preferred_element_type=jnp.float32,
    )
    own_cols = magnitude.shape[0]
    first_col = data_rank * own_cols
    grad_own = lax.psum_scatter(
        weight_grad.astype(jnp.bfloat16), "dp", scatter_dimension=1, tiled=True
    ).astype(jnp.float32)
    direction_own = lax.dynamic_slice_in_dim(direction, first_col, own_cols, 1)
    norm_own = lax.dynamic_slice_in_dim(column_norm, first_col, own_cols, 0)
    scaled_grad = grad_own * (magnitude / norm_own)
    magnitude_part = jnp.sum(grad_own * direction_own, 0) / norm_own
    up_part = jnp.dot(dora_a.T, scaled_grad, precision=lax.Precision.HIGHEST)
    grad_magnitude, grad_b = (
        lax.psum(magnitude_part.astype(jnp.bfloat16), "seq").astype(jnp.float32),
        lax.psum(up_part.astype(jnp.bfloat16), "seq").astype(jnp.float32),
    )
    down_part = jnp.dot(scaled_grad, dora_b.T, precision=lax.Precision.HIGHEST)
    grad_a = lax.psum(down_part.astype(jnp.bfloat16), "dp").astype(jnp.float32)
    return (image_out, grad_a, grad_b, grad_magnitude)


def solution(mesh):
    return jax.shard_map(
        on_device,
        mesh=mesh,
        in_specs=(
            P("dp", None, None),
            P(),
            P(),
            P(),
            P(None, None, "seq"),
            P("seq", None),
            P(),
            P("seq", "dp"),
            P("dp", None),
            P("dp", None),
            P("dp", None, "seq"),
            P(),
            P("dp", "seq", None, None),
            P(),
            P("seq", "dp"),
            P("seq", None),
            P(None, "dp"),
            P("dp"),
            P("dp", "seq", None),
        ),
        out_specs=(P("dp", "seq", None), P("seq", None), P(None, "dp"), P("dp")),
        check_vma=False,
    )
```

profile of v0, /device:TPU:0, one launch (start us, length us, event | category | flops | bytes accessed | tf_op | source)
XLA Modules:
  0.0 512.2 jit_solution(14385898142700955304)
XLA Ops:
  10.2 8.9 %fusion.41 = f32[256,1280]{1,0:T(8,128)} fusion(bf16[2,4096,1280]{2,1,0:T(8,128)(2,1)} %param.23, bf16[1,256,4096]{2,1,0:T(8,128)(2,1)} %param.19, f32[4096]{0:T(1024)} %param.22, f32[256]{0:T(256)S(1)} %add_rsqrt_fusion.3), kind=kOutput, calls=%fused_computation.59 | convolution fusion | flops 2691170304 | bytes 13911040 | tf_op jit(solution)/shard_map/dot_general | solution.py:51
  19.1 15.5 %convolution_convert_fusion = bf16[256,4096]{1,0:T(8,128)(2,1)} fusion(bf16[1280,4096]{1,0:T(8,128)(2,1)} %param.24, f32[256,1280]{1,0:T(8,128)} %fusion.41, bf16[2,4096,1280]{2,1,0:T(8,128)(2,1)} %param.23, bf16[1,256,4096]{2,1,0:T(8,128)(2,1)S(1)} %copy-done.2, f32[4096]{0:T(1024)S(1)} %copy-done.8, f32[256]{0:T(256)S(1)} %add_rsqrt_fusion.3), kind=kOutput, calls=%fused_computation.14 | convolution fusion | flops 5374607360 | bytes 26493952 | tf_op jit(solution)/shard_map/dot_general | solution.py:55
  36.0 45.2 %reduce-scatter.7.cloned.1.call-done = bf16[256,1024]{1,0:T(8,128)(2,1)} async-done(((bf16[256,4096]{1,0:T(8,128)(2,1)}), bf16[256,1024]{1,0:T(8,128)(2,1)}) %reduce-scatter.7.cloned.1.call-update) | async-done | bytes 524304 | tf_op jit(solution)/shard_map/reduce_scatter | solution.py:54
  81.1 5.1 all-gather.10.cloned.1.call-done
  86.2 5.9 %convolution_convert_fusion.2 = bf16[256,3072]{1,0:T(8,128)(2,1)} fusion(bf16[1024,3072]{1,0:T(8,128)(2,1)} %all-gather.10.cloned.1.call-done, bf16[256,1024]{1,0:T(8,128)(2,1)} %reduce-scatter.7.cloned.1.call-done, f32[1024]{0:T(1024)S(1)} %dynamic_slice.16, bf16[1,256,4096]{2,1,0:T(8,128)(2,1)S(1)} %copy-done.2, s32[]{:T(128)S(6)} %select_n.25), kind=kOutput, calls=%fused_computation.22 | convolution fusion | flops 1612709888 | bytes 8916996 | tf_op jit(solution)/shard_map/dot_general | solution.py:61
  92.2 35.5 %reduce-scatter.9.cloned.1.call-done = bf16[64,3072]{1,0:T(8,128)(2,1)} async-done(((bf16[256,3072]{1,0:T(8,128)(2,1)}), bf16[64,3072]{1,0:T(8,128)(2,1)}) %reduce-scatter.9.cloned.1.call-update) | async-done | bytes 393232 | tf_op jit(solution)/shard_map/reduce_scatter | solution.py:66
  129.7 29.1 %all-gather.18.cloned.1.call-done = bf16[512,3072]{1,0:T(8,128)(2,1)} async-done(((bf16[64,3072]{1,0:T(8,128)(2,1)}), bf16[512,3072]{1,0:T(8,128)(2,1)}) %all-gather.18.cloned.1.call-update) | async-done | bytes 3145744 | tf_op jit(solution)/shard_map/all_gather | solution.py:71
  167.5 4.7 all-to-all-start
  175.2 92.6 %all-to-all-done = bf16[128,3,3072]{0,1,2:T(4,128)(2,1)S(1)} async-done(((bf16[128,3,3072]{0,1,2:T(4,128)(2,1)}), bf16[128,3,3072]{0,1,2:T(4,128)(2,1)S(1)}, u32[]{:S(2)}, u32[]{:S(2)}) %all-to-all-start) | async-done | bytes 2359328 | tf_op jit(solution)/shard_map/all_to_all | solution.py:94
  279.7 23.7 %copy.47 = bf16[3072,2,768]{0,2,1:T(8,128)(2,1)} copy(bf16[3072,2,768]{2,1,0:T(2,128)(2,1)} %all-gather.14.cloned.1.call-done) | data formatting | bytes 18874368 | tf_op jit(solution)/shard_map/reshape | solution.py:88
  303.5 5.8 %fusion.29 = f32[256,2,6,128]{0,3,2,1:T(8,128)S(1)} fusion(bf16[2,6,128,3072]{3,2,1,0:T(8,128)(2,1)} %bitcast.115, bf16[256,3072]{1,0:T(8,128)(2,1)} %all-gather.12.cloned.1.call-done), kind=kOutput, calls=%fused_computation.44 | convolution fusion | flops 2415919104 | bytes 12582912 | tf_op jit(solution)/shard_map/dot_general | solution.py:86
  313.8 18.2 %all-gather.20.cloned.1.call-done = bf16[1,512,3072]{2,1,0:T(8,128)(2,1)} async-done(((bf16[1,128,3072]{2,1,0:T(8,128)(2,1)}), bf16[1,512,3072]{2,1,0:T(8,128)(2,1)}) %all-gather.20.cloned.1.call-update) | async-done | bytes 3145744 | tf_op jit(solution)/shard_map/all_gather | solution.py:163
  332.0 6.1 %convolution_convert_fusion.1 = bf16[768,3072]{1,0:T(8,128)(2,1)} fusion(bf16[512,768]{0,1:T(8,128)(2,1)S(1)} %bitcast.120, bf16[1,512,3072]{2,1,0:T(8,128)(2,1)} %all-gather.20.cloned.1.call-done), kind=kOutput, calls=%fused_computation.15 | convolution fusion | flops 2418278400 | bytes 8650752 | tf_op jit(solution)/shard_map/th,td->hd/dot_general | solution.py:160
  338.1 6.7 %copy.48 = bf16[768,3072]{0,1:T(8,128)(2,1)} copy(bf16[768,3072]{1,0:T(8,128)(2,1)} %convolution_convert_fusion.1) | data formatting | bytes 9437184
  345.7 8.8 %all-gather.2 = bf16[8,1,384]{2,1,0:T(2,128)(2,1)S(1)} all-gather(bf16[1,1,384]{2,1,0:T(2,128)(2,1)S(1)} %reshape.135), channel_id=1, replica_groups=mesh['dp'=8,'seq'=4] {'dp'}, dimensions={0}, use_global_device_ids=true | all-gather | bytes 6912 | tf_op jit(solution)/shard_map/all_gather | solution.py:141
  354.6 12.7 %all_gather.29 = bf16[64,3072]{1,0:T(8,128)(2,1)S(1)} all-gather(bf16[64,384]{1,0:T(8,128)(2,1)S(1)} %convert_element_type.152), channel_id=1, replica_groups=mesh['dp'=8,'seq'=4] {'dp'}, dimensions={1}, use_global_device_ids=true | all-gather | bytes 442368 | tf_op jit(solution)/shard_map/all_gather | solution.py:140
  367.3 6.2 %all-gather.16.cloned.1.call-done = bf16[768,3072]{1,0:T(8,128)(2,1)} async-done(((bf16[768,384]{1,0:T(8,128)(2,1)}), bf16[768,3072]{1,0:T(8,128)(2,1)}) %all-gather.16.cloned.1.call-update) | async-done | bytes 4718608 | tf_op jit(solution)/shard_map/all_gather | solution.py:138
  373.5 8.8 %multiply_reduce_fusion = (f32[3072]{0:T(1024)S(1)}, f32[768,3072]{1,0:T(8,128)}) fusion(f32[768,64]{0,1:T(8,128)S(1)} %copy-done, bf16[64,3072]{1,0:T(8,128)(2,1)S(1)} %all_gather.29, bf16[768,3072]{1,0:T(8,128)(2,1)} %all-gather.16.cloned.1.call-done), kind=kOutput, calls=%fused_computation.7 | convolution fusion | flops 1821373440 | bytes 14757888 | tf_op jit(solution)/shard_map/dot_general | solution.py:145
  382.3 18.7 %psum.28 = f32[3072]{0:T(1024)S(1)} all-reduce(f32[3072]{0:T(1024)S(1)} %get-tuple-element.42), channel_id=1, replica_groups=mesh['dp'=8,'seq'=4] {'seq'}, use_global_device_ids=true, to_apply=%region_14.15 | all-reduce | flops 3072 | bytes 24576 | tf_op jit(solution)/shard_map/psum | solution.py:148
  401.0 29.5 %reduce-scatter.13.cloned.1.call-done = bf16[384,768]{1,0:T(8,128)(2,1)} async-done(((bf16[3072,768]{1,0:T(8,128)(2,1)}), bf16[384,768]{1,0:T(8,128)(2,1)}) %reduce-scatter.13.cloned.1.call-update) | async-done | bytes 589840
  435.4 7.7 %fusion.9 = bf16[512,3072]{1,0:T(8,128)(2,1)} fusion(bf16[512,768]{0,1:T(8,128)(2,1)S(1)} %bitcast.121, f32[768,3072]{1,0:T(8,128)} %get-tuple-element.43, f32[3072]{0:T(1024)S(1)} %get-tuple-element.35), kind=kOutput, calls=%fused_computation.18 | convolution fusion | flops 2422210560 | bytes 13381632 | tf_op jit(solution)/shard_map/dot_general | solution.py:154
  444.1 22.0 %all-reduce = (bf16[64,384]{1,0:T(8,128)(2,1)S(1)}, bf16[384]{0:T(512)(128)(2,1)S(1)}) all-reduce(bf16[64,384]{1,0:T(8,128)(2,1)S(1)} %fusion.49, bf16[384]{0:T(512)(128)(2,1)S(1)} %get-tuple-element.32), channel_id=1, replica_groups=mesh['dp'=8,'seq'=4] {'seq'}, use_global_device_ids=true, to_apply=%region_18.19 | all-reduce | flops 24960 | bytes 99840 | tf_op jit(solution)/shard_map/psum | solution.py:178
  467.3 19.7 %all-reduce.3.cloned.1.call-done = bf16[768,64]{0,1:T(8,128)(2,1)} async-done(((bf16[768,64]{0,1:T(8,128)(2,1)}), bf16[768,64]{0,1:T(8,128)(2,1)}) %all-reduce.3.cloned.1.call-update) | async-done | bytes 98320 | tf_op jit(solution)/shard_map/psum | solution.py:181
  488.6 16.5 %reduce-scatter.11.cloned.1.call-done = bf16[128,3072]{1,0:T(8,128)(2,1)} async-done(((bf16[512,3072]{1,0:T(8,128)(2,1)}), bf16[128,3072]{1,0:T(8,128)(2,1)}) %reduce-scatter.11.cloned.1.call-update) | async-done | bytes 786448 | tf_op jit(solution)/shard_map/reduce_scatter | solution.py:153
  (94 shorter events, 43.1 us)
Async XLA Ops:
  8.0 365.5 %copy-start = (f32[768,64]{0,1:T(8,128)S(1)}, f32[768,64]{0,1:T(8,128)}, u32[]{:S(2)}) copy-start(f32[768,64]{0,1:T(8,128)} %param.34) | copy-start | bytes 589828
  8.0 73.1 %reduce-scatter.7.cloned.1.call-start = ((), (), s32[]{:S(2)}) async-start(), calls=%async_computation.5 | async-start | bytes 2621440 | tf_op jit(solution)/shard_map/reduce_scatter | solution.py:54
  10.2 8.9 %copy-start.2 = (bf16[1,256,4096]{2,1,0:T(8,128)(2,1)S(1)}, bf16[1,256,4096]{2,1,0:T(8,128)(2,1)}, u32[]{:S(2)}) copy-start(bf16[1,256,4096]{2,1,0:T(8,128)(2,1)} %param.19) | copy-start | bytes 6291460
  10.2 8.9 %copy-start.8 = (f32[4096]{0:T(1024)S(1)}, f32[4096]{0:T(1024)}, u32[]{:S(2)}) copy-start(f32[4096]{0:T(1024)} %param.22) | copy-start | bytes 49156
  34.6 51.6 %all-gather.10.cloned.1.call-start = ((), (), s32[]{:S(2)}) async-start(), calls=%async_computation.6 | async-start | bytes 7077888 | tf_op jit(solution)/shard_map/all_gather | solution.py:63
  35.2 92.5 %reduce-scatter.9.cloned.1.call-start = ((), (), s32[]{:S(2)}) async-start(), calls=%async_computation.7 | async-start | bytes 1966080 | tf_op jit(solution)/shard_map/reduce_scatter | solution.py:66
  92.1 36.3 %copy-start.9 = (s32[8]{0:T(128)S(1)}, s32[8]{0:T(128)}, u32[]{:S(2)}) copy-start(s32[8]{0:T(128)} %param.21) | copy-start | bytes 100
  92.1 37.6 %copy-start.4 = (f32[1,3072]{1,0:T(1,128)S(1)}, f32[1,3072]{1,0:T(1,128)}, u32[]{:S(2)}) copy-start(f32[1,3072]{1,0:T(1,128)} %param.28) | copy-start | bytes 36868
  92.1 70.0 %copy-start.5 = (f32[1,3072]{1,0:T(1,128)S(1)}, f32[1,3072]{1,0:T(1,128)}, u32[]{:S(2)}) copy-start(f32[1,3072]{1,0:T(1,128)} %param.27) | copy-start | bytes 36868
  92.1 66.6 %all-gather.18.cloned.1.call-start = ((), (), s32[]{:S(2)}) async-start(), calls=%async_computation.13 | async-start | bytes 3538944 | tf_op jit(solution)/shard_map/all_gather | solution.py:71
  127.7 152.0 %all-gather.14.cloned.1.call-start = ((), (), s32[]{:S(2)}) async-start(), calls=%async_computation.9 | async-start | bytes 10616832 | tf_op jit(solution)/shard_map/all_gather | solution.py:85
  128.3 175.2 %all-gather.12.cloned.1.call-start = ((), (), s32[]{:S(2)}) async-start(), calls=%async_computation.8 | async-start | bytes 1966080 | tf_op jit(solution)/shard_map/all_gather | solution.py:82
  158.8 5.1 copy-start.1
  163.1 168.9 %all-gather.20.cloned.1.call-start = ((), (), s32[]{:S(2)}) async-start(), calls=%async_computation.14 | async-start | bytes 3932160 | tf_op jit(solution)/shard_map/all_gather | solution.py:163
  167.5 5.7 %copy-start.10 = (s32[8]{0:T(128)S(1)}, s32[8]{0:T(128)}, u32[]{:S(2)}) copy-start(s32[8]{0:T(128)} %param.20) | copy-start | bytes 100
  167.5 7.6 %copy-start.7 = (f32[2,128]{1,0:T(2,128)S(1)}, f32[2,128]{1,0:T(2,128)}, u32[]{:S(2)}) copy-start(f32[2,128]{1,0:T(2,128)} %param.32) | copy-start | bytes 3076
  167.5 100.3 %all-to-all-start = ((bf16[128,3,3072]{0,1,2:T(4,128)(2,1)}), bf16[128,3,3072]{0,1,2:T(4,128)(2,1)S(1)}, u32[]{:S(2)}, u32[]{:S(2)}) async-start(bf16[128,3,3072]{0,1,2:T(4,128)(2,1)} %bitcast.114), calls=%async_computation.2 | async-start | bytes 6291456 | tf_op jit(solution)/shard_map/all_to_all | solution.py:94
  172.2 201.3 %all-gather.16.cloned.1.call-start = ((), (), s32[]{:S(2)}) async-start(), calls=%async_computation.10 | async-start | bytes 5308416 | tf_op jit(solution)/shard_map/all_gather | solution.py:138
  173.0 257.5 %reduce-scatter.13.cloned.1.call-start = ((), (), s32[]{:S(2)}) async-start(), calls=%async_computation.15 | async-start | bytes 5308416
  303.5 5.9 %copy-start.11 = (f32[128]{0:T(128)S(1)}, f32[128]{0:T(128)}, u32[]{:S(2)}) copy-start(f32[128]{0:T(128)} %param.30) | copy-start | bytes 1540
  309.4 2.2 slice-start
  310.4 2.1 slice-start.1
  344.8 142.2 %all-reduce.3.cloned.1.call-start = ((), (), s32[]{:S(2)}) async-start(), calls=%async_computation.12 | async-start | bytes 196608 | tf_op jit(solution)/shard_map/psum | solution.py:181
  435.4 69.7 %reduce-scatter.11.cloned.1.call-start = ((), (), s32[]{:S(2)}) async-start(), calls=%async_computation.11 | async-start | bytes 3932160 | tf_op jit(solution)/shard_map/reduce_scatter | solution.py:153
  (2 other events, 1.8 us)
Sparse Core Ops, SparseCore 0:
  34.8 46.3 reduce-scatter.6
  92.3 35.4 reduce-scatter.8
  443.3 61.7 reduce-scatter.10
Sparse Core Ops, SparseCore 1:
  37.0 49.2 all-gather.9
  127.8 30.9 all-gather.17
  160.5 58.6 all-gather.13
  221.4 47.8 all-gather.11
  270.8 61.2 all-gather.19
  333.9 39.6 all-gather.15
  376.8 53.6 reduce-scatter.12
  435.5 51.5 all-reduce.2
where the time goes:
time: 514 us; the launch traced here: 512 us
  waiting for transfers between devices  300 us (58%)
  matrix products  68.6 us (13%)
  blocking collectives  62.2 us (12%)
  local copies, waits for them, and re-layouts  45.9 us (9%)
  between operations  15.6 us (3%)
  other arithmetic  14.5 us (3%)
  starting transfers between devices  5.33 us (1%)
    all_to_all x1, waiting for transfers between devices, on_device(): lax.all_to_all(image_query_key_value[0], 'seq', split_axis=2, concat_axis...  92.6 us
    reduce_scatter x1, waiting for transfers between devices, on_device(): lax.psum_scatter(jnp.dot(hidden, t5_out_weight, preferred_element_type=jn...  45.2 us
    reduce_scatter x1, waiting for transfers between devices, on_device(): lax.psum_scatter(context_part.astype(jnp.bfloat16), 'seq', scatter_dimens...  35.5 us
    unnamed x12, waiting for transfers between devices  32.1 us
    all_gather x1, waiting for transfers between devices, on_device(): shard_piece = lax.all_gather(text_tokens[None], 'dp', axis=0, tiled=True)  29.1 us
    reshape x1, local copies, waits for them, and re-layouts, on_device(): shard_piece.reshape(shard_piece.shape[0], 2 * head_width)  23.7 us
    psum x1, blocking collectives, on_device(): lax.psum(up_part.astype(jnp.bfloat16), 'seq').astype(jnp.float32)  22 us
    psum x1, waiting for transfers between devices, on_device(): grad_a = lax.psum(down_part.astype(jnp.bfloat16), 'dp').astype(jnp.float32)  19.7 us
  transfers between devices with their start and end apart: 12, of which 10 were waited for; matrix products, arithmetic and copies ran while one was open for 17% of the time, Pallas kernels for 0%

commit v1 on v0

v1 whole, which is shorter than its diff:
```python
import functools
import math

import jax
import jax.numpy as jnp
from jax import lax
from jax.experimental import pallas as pl
from jax.experimental.pallas import tpu as pltpu
from jax.sharding import PartitionSpec as P

HD = 128
MAX_PROMPT = 128
EPSILON = 1e-06


def rms_scale(values, gain):
    return values * lax.rsqrt(jnp.mean(values * values, -1, keepdims=True) + EPSILON) * gain


def attention_kernel(blocks, length_ref, text_gain_ref, image_gain_ref, text_key_ref, text_value_ref, *refs):
    image_refs, out_ref = refs[:blocks], refs[blocks]

    def stacked(kind):
        return jnp.concatenate([ref[kind] for ref in image_refs], 0)

    queries = rms_scale(stacked(0).astype(jnp.float32), image_gain_ref[0:1, :])
    queries = (queries).astype(jnp.bfloat16)
    key_image = rms_scale(stacked(1).astype(jnp.float32), image_gain_ref[1:2, :]).astype(jnp.bfloat16)
    key_text = rms_scale(text_key_ref[...], text_gain_ref[...]).astype(jnp.bfloat16)
    scale = 1.0 / math.sqrt(HD)
    dims = (((1,), (1,)), ((), ()))
    text_scores = lax.dot_general(queries, key_text, dims, preferred_element_type=jnp.float32) * scale
    image_scores = lax.dot_general(queries, key_image, dims, preferred_element_type=jnp.float32) * scale
    position = lax.broadcasted_iota(jnp.int32, text_scores.shape, 1)
    text_weight = jnp.where(position < length_ref[0], jnp.exp(text_scores), 0.0)
    image_weight = jnp.exp(image_scores)
    denominator = jnp.sum(text_weight, -1, keepdims=True) + jnp.sum(image_weight, -1, keepdims=True)
    mixture = jnp.dot(
        text_weight.astype(jnp.bfloat16),
        text_value_ref[...].astype(jnp.bfloat16),
        preferred_element_type=jnp.float32,
    )
    mixture = mixture + jnp.dot(
        image_weight.astype(jnp.bfloat16), stacked(2), preferred_element_type=jnp.float32
    )
    out_ref[...] = (mixture / denominator).astype(jnp.bfloat16)


def attention(length, text_gain, image_gain, key_value, image_blocks):
    blocks = len(image_blocks)
    _, rows, width = image_blocks[0].shape
    heads = width // HD
    text = key_value.shape[0]
    vmem = lambda shape, index: pl.BlockSpec(shape, index)
    return pl.pallas_call(
        functools.partial(attention_kernel, blocks),
        grid=(heads,),
        out_shape=jax.ShapeDtypeStruct((blocks * rows, width), jnp.bfloat16),
        in_specs=[
            pl.BlockSpec(memory_space=pltpu.SMEM),
            vmem((1, HD), lambda h: (0, 0)),
            vmem((2, HD), lambda h: (0, 0)),
            vmem((text, HD), lambda h: (0, h)),
            vmem((text, HD), lambda h: (0, heads + h)),
        ]
        + [vmem((3, rows, HD), lambda h: (0, 0, h))] * blocks,
        out_specs=vmem((blocks * rows, HD), lambda h: (0, h)),
        cost_estimate=pl.CostEstimate(
            flops=4 * heads * blocks * rows * (blocks * rows + text) * HD,
            bytes_accessed=8 * blocks * rows * width,
            transcendentals=heads * blocks * rows * (blocks * rows + text),
        ),
    )(length.reshape(1), text_gain.reshape(1, HD), image_gain, key_value, key_value, *image_blocks)


def on_device(
    enc_states,
    lengths,
    prompt_owner_sample,
    t5_gain,
    t5_in_weight,
    t5_out_weight,
    t5_final_gain,
    context_weight,
    text_shift,
    text_scale,
    kv_weight,
    text_key_gain,
    image_query_key_value,
    image_qk_gain,
    proj_weight,
    dora_a,
    dora_b,
    magnitude,
    grad_out,
):
    seq_rank = lax.axis_index("seq")
    data_rank = lax.axis_index("dp")
    seq_devices = lax.axis_size("seq")
    bf16, f32 = jnp.bfloat16, jnp.float32

    def shifted(values, step):
        return lax.ppermute(values, "seq", [(i, (i + step) % seq_devices) for i in range(seq_devices)])

    image_rows = jnp.transpose(image_query_key_value[0], (1, 0, 2))
    head_width = image_rows.shape[2] // seq_devices

    def heads_of(rank):
        return lax.dynamic_slice_in_dim(image_rows, rank * head_width, head_width, 2)

    image_blocks = [heads_of(seq_rank)] + [
        shifted(heads_of((seq_rank + k) % seq_devices), k) for k in range(1, seq_devices)
    ]

    direction = proj_weight.astype(f32) + jnp.dot(dora_a, dora_b, precision=lax.Precision.HIGHEST)
    column_norm = jnp.sqrt(lax.psum(jnp.sum(direction * direction, 0), "seq") + EPSILON)
    ratio = magnitude / column_norm
    gathered = lax.all_gather(
        jnp.concatenate([(direction * ratio).astype(bf16), (dora_b * ratio).astype(bf16)], 0),
        "dp",
        axis=1,
        tiled=True,
    )
    scaled, scaled_up = gathered[: dora_a.shape[0]], gathered[dora_a.shape[0] :]

    tokens = enc_states[0, :MAX_PROMPT]
    text_length, width_enc = tokens.shape
    feat_width = width_enc // seq_devices
    own_tokens = lax.dynamic_slice_in_dim(tokens, seq_rank * feat_width, feat_width, 1).astype(f32)
    own_final = lax.dynamic_slice_in_dim(t5_final_gain, seq_rank * feat_width, feat_width, 0)
    normed = rms_scale(tokens.astype(f32), t5_gain).astype(bf16)
    gate_proj = jnp.dot(normed, t5_in_weight[0], preferred_element_type=f32)
    upward = jnp.dot(normed, t5_in_weight[1], preferred_element_type=f32)
    hidden = (jax.nn.gelu(gate_proj, approximate=True) * upward).astype(bf16)
    ffn_part = lax.psum_scatter(
        jnp.dot(hidden, t5_out_weight, preferred_element_type=f32).astype(bf16),
        "seq",
        scatter_dimension=1,
        tiled=True,
    ).astype(f32)
    encoded = ((own_tokens + ffn_part) * own_final).astype(bf16)
    context_part = jnp.dot(
        encoded,
        lax.all_gather(context_weight, "dp", axis=1, tiled=True),
        preferred_element_type=f32,
    )
    text_tokens = lax.psum_scatter(context_part.astype(bf16), "seq", scatter_dimension=0, tiled=True)
    routes = prompt_owner_sample == data_rank
    diffusion_length = jnp.sum(jnp.where(routes, lengths, 0))
    prompts = lax.all_gather(text_tokens[None], "dp", axis=0, tiled=True)
    routed = jnp.sum(jnp.where(routes[:, None, None], prompts, jnp.zeros_like(prompts)), 0).astype(f32)
    centre = jnp.mean(routed, -1, keepdims=True)
    spread = jnp.mean((routed - centre) * (routed - centre), -1, keepdims=True)
    layer_normed = (routed - centre) * lax.rsqrt(spread + EPSILON)
    modulated = ((1.0 + text_scale) * layer_normed + text_shift).astype(bf16)
    text_all = lax.all_gather(modulated, "seq", axis=0, tiled=True)
    kv_rows = lax.all_gather(kv_weight.reshape(kv_weight.shape[0], -1), "dp", axis=0, tiled=True)
    key_value = jnp.dot(text_all, kv_rows, preferred_element_type=f32)

    attended = attention(diffusion_length, text_key_gain, image_qk_gain, key_value, image_blocks)

    rows = image_rows.shape[1]
    up_rows = jnp.dot(attended, dora_a.astype(bf16), preferred_element_type=f32).astype(bf16)
    down = lax.dot_general(
        grad_out[0], scaled_up, (((1,), (1,)), ((), ())), preferred_element_type=f32
    ).astype(bf16)
    down_rows = jnp.concatenate([down] + [shifted(down, k) for k in range(1, seq_devices)], 0)
    total, up_total = 0.0, 0.0
    for k in list(range(1, seq_devices)) + [0]:
        block = attended[k * rows : (k + 1) * rows]
        part = jnp.dot(block, scaled, preferred_element_type=f32).astype(bf16)
        up_part = up_rows[k * rows : (k + 1) * rows]
        if k:
            part, up_part = shifted(part, seq_devices - k), shifted(up_part, seq_devices - k)
        total, up_total = total + part.astype(f32), up_total + up_part.astype(f32)
    image_out = total.astype(bf16)

    grad_a = lax.psum(
        lax.dot_general(
            attended, down_rows, (((0,), (0,)), ((), ())), preferred_element_type=f32
        ).astype(bf16),
        "dp",
    ).astype(f32)
    grad_up = lax.dot_general(
        up_total.astype(bf16), grad_out[0], (((0,), (0,)), ((), ())), preferred_element_type=f32
    )
    grad_size = jnp.sum(grad_out[0].astype(f32) * total, 0, keepdims=True)
    column_parts = lax.psum_scatter(
        jnp.concatenate([grad_up, grad_size], 0).astype(bf16), "dp", scatter_dimension=1, tiled=True
    )
    column_sums = lax.psum(column_parts, "seq").astype(f32)
    rank = dora_b.shape[0]
    grad_b = column_sums[:rank] * ratio
    grad_magnitude = column_sums[rank] / magnitude
    return (image_out[None], grad_a, grad_b, grad_magnitude)


def solution(mesh):
    return jax.shard_map(
        on_device,
        mesh=mesh,
        in_specs=(
            P("dp", None, None),
            P(),
            P(),
            P(),
            P(None, None, "seq"),
            P("seq", None),
            P(),
            P("seq", "dp"),
            P("dp", None),
            P("dp", None),
            P("dp", None, "seq"),
            P(),
            P("dp", "seq", None, None),
            P(),
            P("seq", "dp"),
            P("seq", None),
            P(None, "dp"),
            P("dp"),
            P("dp", "seq", None),
        ),
        out_specs=(P("dp", "seq", None), P("seq", None), P(None, "dp"), P("dp")),
        check_vma=False,
    )
```

time: 514 us -> 438 us (0.85)
  waiting for transfers between devices: 300 us -> 259 us
  local copies, waits for them, and re-layouts: 45.9 us -> 7.95 us
  starting transfers between devices: 5.33 us -> 38.1 us
  matrix products: 68.6 us -> 49.1 us
  blocking collectives: 62.2 us -> 51.4 us
  Pallas kernels: 0 us -> 7.85 us
  other arithmetic: 14.5 us -> 8.29 us
    all_to_all x1 -> x0, waiting for transfers between devices: 92.6 us -> none  [on_device(): lax.all_to_all(image_query_key_value[0], 'seq', split_axis=2, concat_axis...]
    reduce_scatter x3 -> x2, waiting for transfers between devices: 97.2 us -> 37.9 us  [the longest x1 28.8 us: on_device(): lax.psum_scatter(jnp.dot(hidden, t5_out_weight, preferred_element_type=f3...]
    ppermute x0 -> x12, waiting for transfers between devices: none -> 38.8 us  [shifted(): lax.ppermute(values, 'seq', [(i, (i + step) % seq_devices) for i in range...]
    ppermute x0 -> x12, starting transfers between devices: none -> 37.8 us  [shifted(): lax.ppermute(values, 'seq', [(i, (i + step) % seq_devices) for i in range...]
    reshape x2 -> x0, local copies, waits for them, and re-layouts: 27.8 us -> none  [the longest x1 23.7 us: on_device(): shard_piece.reshape(shard_piece.shape[0], 2 * head_width)]
    all_gather x5 -> x3, waiting for transfers between devices: 53.4 us -> 81.2 us  [the longest x1 38.5 us: on_device(): lax.all_gather(kv_weight.reshape(kv_weight.shape[0], -1), 'dp', axis=0, t...]
    psum x1, waiting for transfers between devices: 19.7 us -> 41.8 us  [on_device(): lax.psum(lax.dot_general(attended, down_rows, (((0,), (0,)), ((), ())), p...]
    dot_general x12, matrix products: 62.7 us -> 44.4 us  [the longest x4 17.1 us: on_device(): part = jnp.dot(block, scaled, preferred_element_type=f32).astype(bf16)]
  transfers between devices with their start and end apart: 12 -> 20, of which waited for: 10 -> 10; matrix products, arithmetic and copies ran while one was open for 17% -> 9% of each run, Pallas kernels for 0% -> 2%
where the time goes in v1:
time: 438 us
  waiting for transfers between devices  259 us (59%)
  blocking collectives  51.4 us (12%)
  matrix products  49.1 us (11%)
  starting transfers between devices  38.1 us (9%)
  between operations  15.9 us (4%)
  other arithmetic  8.29 us (2%)
  local copies, waits for them, and re-layouts  7.95 us (2%)
  Pallas kernels  7.85 us (2%)
    psum x1, waiting for transfers between devices, on_device(): lax.psum(lax.dot_general(attended, down_rows, (((0,), (0,)), ((), ())), p...  41.8 us
    ppermute x12, waiting for transfers between devices, shifted(): lax.ppermute(values, 'seq', [(i, (i + step) % seq_devices) for i in range...  38.8 us
    all_gather x1, waiting for transfers between devices, on_device(): lax.all_gather(kv_weight.reshape(kv_weight.shape[0], -1), 'dp', axis=0, t...  38.5 us
    unnamed x9, waiting for transfers between devices  38 us
    ppermute x12, starting transfers between devices, shifted(): lax.ppermute(values, 'seq', [(i, (i + step) % seq_devices) for i in range...  37.8 us
    reduce_scatter x1, waiting for transfers between devices, on_device(): lax.psum_scatter(jnp.dot(hidden, t5_out_weight, preferred_element_type=f3...  28.8 us
    all_gather x1, waiting for transfers between devices, on_device(): prompts = lax.all_gather(text_tokens[None], 'dp', axis=0, tiled=True)  21.9 us
    all_gather x1, waiting for transfers between devices, on_device(): lax.all_gather(context_weight, 'dp', axis=1, tiled=True)  21.4 us
  transfers between devices with their start and end apart: 20, of which 10 were waited for; matrix products, arithmetic and copies ran while one was open for 9% of the time, Pallas kernels for 2%

profile of v1, /device:TPU:0, one launch (start us, length us, event | category | flops | bytes accessed | tf_op | source)
XLA Modules:
  0.0 437.7 jit_solution(11443033216402739578)
XLA Ops:
  9.6 5.6 %fusion.32 = f32[128,1280]{1,0:T(8,128)S(1)} fusion(bf16[2,4096,1280]{2,1,0:T(8,128)(2,1)} %param.23, f32[4096]{0:T(1024)} %param.22, f32[128]{0:T(128)S(1)} %add_rsqrt_fusion.1, bf16[1,256,4096]{2,1,0:T(8,128)(2,1)} %param.19), kind=kOutput, calls=%fused_computation.46 | convolution fusion | flops 1345585152 | bytes 12206592 | tf_op jit(solution)/shard_map/dot_general | solution.py:132
  15.2 11.5 %convolution_convert_fusion = bf16[128,4096]{1,0:T(8,128)(2,1)} fusion(bf16[1280,4096]{1,0:T(8,128)(2,1)} %param.24, f32[128,1280]{1,0:T(8,128)S(1)} %fusion.32, bf16[2,4096,1280]{2,1,0:T(8,128)(2,1)} %param.23, f32[4096]{0:T(1024)S(1)} %copy-done.14, f32[128]{0:T(128)S(1)} %add_rsqrt_fusion.1, bf16[1,256,4096]{2,1,0:T(8,128)(2,1)S(1)} %copy-done.3), kind=kOutput, calls=%fused_computation.6 | convolution fusion | flops 2687303680 | bytes 23740928 | tf_op jit(solution)/shard_map/dot_general | solution.py:136
  28.1 28.8 %reduce-scatter.6.cloned.1.call-done = bf16[128,1024]{1,0:T(8,128)(2,1)} async-done(((bf16[128,4096]{1,0:T(8,128)(2,1)}), bf16[128,1024]{1,0:T(8,128)(2,1)}) %reduce-scatter.6.cloned.1.call-update) | async-done | bytes 262160 | tf_op jit(solution)/shard_map/reduce_scatter | solution.py:135
  56.9 21.4 %all-gather.6.cloned.1.call-done = bf16[1024,3072]{1,0:T(8,128)(2,1)} async-done(((bf16[1024,384]{1,0:T(8,128)(2,1)}), bf16[1024,3072]{1,0:T(8,128)(2,1)}) %all-gather.6.cloned.1.call-update) | async-done | bytes 6291472 | tf_op jit(solution)/shard_map/all_gather | solution.py:144
  78.3 4.8 %convolution_convert_fusion.5 = bf16[128,3072]{1,0:T(8,128)(2,1)} fusion(bf16[1024,3072]{1,0:T(8,128)(2,1)} %all-gather.6.cloned.1.call-done, bf16[128,1024]{1,0:T(8,128)(2,1)} %reduce-scatter.6.cloned.1.call-done, f32[1024]{0:T(1024)S(1)} %dynamic_slice.19, bf16[1,128,4096]{2,1,0:T(8,128)(2,1)S(1)} %slice-done, s32[]{:T(128)S(6)} %select_n.40), kind=kOutput, calls=%fused_computation.12 | convolution fusion | flops 806354944 | bytes 7606276 | tf_op jit(solution)/shard_map/dot_general | solution.py:142
  84.4 12.0 %psum.21 = f32[384]{0:T(512)S(1)} all-reduce(f32[384]{0:T(512)S(1)} %get-tuple-element.15), channel_id=1, replica_groups=mesh['dp'=8,'seq'=4] {'seq'}, use_global_device_ids=true, to_apply=%region_8.9 | all-reduce | flops 384 | bytes 3072 | tf_op jit(solution)/shard_map/psum | solution.py:116
  97.6 9.0 %reduce-scatter.8.cloned.1.call-done = bf16[32,3072]{1,0:T(8,128)(2,1)} async-done(((bf16[128,3072]{1,0:T(8,128)(2,1)}), bf16[32,3072]{1,0:T(8,128)(2,1)}) %reduce-scatter.8.cloned.1.call-update) | async-done | bytes 196624 | tf_op jit(solution)/shard_map/reduce_scatter | solution.py:147
  115.3 20.8 %all-gather.10.cloned.1.call-done = bf16[832,3072]{1,0:T(8,128)(2,1)} async-done(((bf16[832,384]{1,0:T(8,128)(2,1)}), bf16[832,3072]{1,0:T(8,128)(2,1)}) %all-gather.10.cloned.1.call-update) | async-done | bytes 5111824 | tf_op jit(solution)/shard_map/all_gather | solution.py:118
  141.4 21.9 %all-gather.12.cloned.1.call-done = bf16[256,3072]{1,0:T(8,128)(2,1)} async-done(((bf16[32,3072]{1,0:T(8,128)(2,1)}), bf16[256,3072]{1,0:T(8,128)(2,1)}) %all-gather.12.cloned.1.call-update) | async-done | bytes 1572880 | tf_op jit(solution)/shard_map/all_gather | solution.py:150
  165.5 19.7 %all_gather.17 = bf16[128,3072]{1,0:T(8,128)(2,1)S(1)} all-gather(bf16[32,3072]{1,0:T(8,128)(2,1)S(1)} %fusion.42), channel_id=1, replica_groups=mesh['dp'=8,'seq'=4] {'seq'}, dimensions={0}, use_global_device_ids=true | all-gather | bytes 983040 | tf_op jit(solution)/shard_map/all_gather | solution.py:156
  185.3 38.5 %all-gather.8.cloned.1.call-done = bf16[3072,1536]{1,0:T(8,128)(2,1)} async-done(((bf16[384,1536]{1,0:T(8,128)(2,1)}), bf16[3072,1536]{1,0:T(8,128)(2,1)}) %all-gather.8.cloned.1.call-update) | async-done | bytes 9437200 | tf_op jit(solution)/shard_map/all_gather | solution.py:157
  223.8 6.0 %fusion.78.text_key_ref.text_value_ref = f32[128,1536]{1,0:T(8,128)} fusion(bf16[128,3072]{1,0:T(8,128)(2,1)S(1)} %all_gather.17, bf16[3072,1536]{1,0:T(8,128)(2,1)} %all-gather.8.cloned.1.call-done), kind=kOutput, calls=%fused_computation.97 | convolution fusion | flops 1207959552 | bytes 11010048 | tf_op jit(solution)/shard_map/dot_general | solution.py:158
  230.8 7.9 %shard_map.210 = bf16[512,768]{1,0:T(8,128)(2,1)} custom-call(s32[1]{0:T(128)} %bitcast.length_ref, f32[1,128]{1,0:T(1,128)} %bitcast.75, f32[2,128]{1,0:T(2,128)} %image_gain_ref.1, f32[128,1536]{1,0:T(8,128)} %fusion.78.text_key_ref.text_value_ref, f32[128,1536]{1,0:T(8,128)} %fusion.78.text_key_ref.text_value_ref, ...), custom_call_target="tpu_custom_call" | custom-call | flops 1006632960 | bytes 3145728 | tf_op jit(solution)/shard_map/pallas_call | solution.py:55
  238.6 4.2 convolution_convert_fusion.4
  242.8 3.3 collective-permute-start.3
  246.2 4.0 convolution_convert_fusion.3
  250.2 4.0 convolution_convert_fusion.2
  259.6 38.3 %collective-permute-done.8 = bf16[128,64]{0,1:T(8,128)(2,1)S(1)} collective-permute-done((bf16[128,64]{0,1:T(8,128)(2,1)S(1)}, bf16[128,64]{0,1:T(8,128)(2,1)S(1)}, u32[]{:S(2)}, u32[]{:S(2)}) %collective-permute-start.8) | collective-permute-done | bytes 16416 | tf_op jit(solution)/shard_map/ppermute | solution.py:103
  297.9 18.1 %collective-permute-start.11 = (bf16[128,64]{0,1:T(8,128)(2,1)S(1)}, bf16[128,64]{0,1:T(8,128)(2,1)S(1)}, u32[]{:S(2)}, u32[]{:S(2)}) collective-permute-start(bf16[128,64]{0,1:T(8,128)(2,1)S(1)} %get-tuple-element.13), channel_id=1, source_target_pairs={{0,1},{1,2},{2,3},{3,0},{4,5},{5,6},{6,7},{7,4},{8,9},{9,10},{10,1... | collective-permute-start | bytes 49160 | tf_op jit(solution)/shard_map/ppermute | solution.py:103
  316.0 3.6 collective-permute-start.9
  321.4 4.9 %multiply_reduce_fusion = (bf16[3072]{0:T(1024)(128)(2,1)S(1)}, bf16[1,128,3072]{2,1,0:T(8,128)(2,1)}) fusion(bf16[1,128,3072]{2,1,0:T(8,128)(2,1)S(1)} %copy-done.1, bf16[832,3072]{1,0:T(8,128)(2,1)} %all-gather.10.cloned.1.call-done, bf16[512,768]{1,0:T(8,128)(2,1)S(1)} %copy-done, bf16[128,3072]{1,0:T(8,128)(2,1)} %collective-permute-done.5, ...), kind=kOutput, calls=%fused_computation.25 | convolution fusion | flops 608695296 | bytes 8853504 | tf_op jit(solution)/shard_map/dot_general | solution.py:171
  327.6 41.8 %all-reduce.2.cloned.1.call-done = bf16[768,64]{0,1:T(8,128)(2,1)} async-done(((bf16[768,64]{0,1:T(8,128)(2,1)}), bf16[768,64]{0,1:T(8,128)(2,1)}) %all-reduce.2.cloned.1.call-update) | async-done | bytes 98320 | tf_op jit(solution)/shard_map/psum | solution.py:178
  371.0 37.4 %reduce-scatter.10.cloned.1.call-done = bf16[384,65]{1,0:T(8,128)(2,1)} async-done(((bf16[3072,65]{1,0:T(8,128)(2,1)}), bf16[384,65]{1,0:T(8,128)(2,1)}) %reduce-scatter.10.cloned.1.call-update) | async-done | bytes 49936
  409.4 19.6 %psum.23 = bf16[65,384]{1,0:T(8,128)(2,1)S(1)} all-reduce(bf16[65,384]{1,0:T(8,128)(2,1)S(1)} %copy.24), channel_id=1, replica_groups=mesh['dp'=8,'seq'=4] {'seq'}, use_global_device_ids=true, to_apply=%region_12.13 | all-reduce | flops 24960 | bytes 99840 | tf_op jit(solution)/shard_map/psum | solution.py:191
  (100 shorter events, 34.6 us)
Async XLA Ops:
  8.0 48.9 %reduce-scatter.6.cloned.1.call-start = ((), (), s32[]{:S(2)}) async-start(), calls=%async_computation.3 | async-start | bytes 1310720 | tf_op jit(solution)/shard_map/reduce_scatter | solution.py:135
  26.8 51.6 %all-gather.6.cloned.1.call-start = ((), (), s32[]{:S(2)}) async-start(), calls=%async_computation.4 | async-start | bytes 7077888 | tf_op jit(solution)/shard_map/all_gather | solution.py:144
  27.4 79.2 %reduce-scatter.8.cloned.1.call-start = ((), (), s32[]{:S(2)}) async-start(), calls=%async_computation.5 | async-start | bytes 983040 | tf_op jit(solution)/shard_map/reduce_scatter | solution.py:147
  28.1 55.1 %copy-start.4 = (f32[768,64]{0,1:T(8,128)S(1)}, f32[768,64]{0,1:T(8,128)}, u32[]{:S(2)}) copy-start(f32[768,64]{0,1:T(8,128)} %param.34) | copy-start | bytes 589828
  28.1 55.1 %copy-start.5 = (bf16[768,384]{1,0:T(8,128)(2,1)S(1)}, bf16[768,384]{1,0:T(8,128)(2,1)}, u32[]{:S(2)}) copy-start(bf16[768,384]{1,0:T(8,128)(2,1)} %param.33) | copy-start | bytes 1769476
  28.1 55.1 %copy-start.8 = (f32[64,384]{1,0:T(8,128)S(1)}, f32[64,384]{1,0:T(8,128)}, u32[]{:S(2)}) copy-start(f32[64,384]{1,0:T(8,128)} %param.35) | copy-start | bytes 294916
  83.1 52.9 %all-gather.10.cloned.1.call-start = ((), (), s32[]{:S(2)}) async-start(), calls=%async_computation.7 | async-start | bytes 5750784 | tf_op jit(solution)/shard_map/all_gather | solution.py:118
  97.5 65.8 %all-gather.12.cloned.1.call-start = ((), (), s32[]{:S(2)}) async-start(), calls=%async_computation.9 | async-start | bytes 1769472 | tf_op jit(solution)/shard_map/all_gather | solution.py:150
  106.6 117.2 %all-gather.8.cloned.1.call-start = ((), (), s32[]{:S(2)}) async-start(), calls=%async_computation.6 | async-start | bytes 10616832 | tf_op jit(solution)/shard_map/all_gather | solution.py:157
  109.2 260.3 %all-reduce.2.cloned.1.call-start = ((), (), s32[]{:S(2)}) async-start(), calls=%async_computation.8 | async-start | bytes 196608 | tf_op jit(solution)/shard_map/psum | solution.py:178
  110.8 54.6 %copy-start.9 = (f32[1,3072]{1,0:T(1,128)S(1)}, f32[1,3072]{1,0:T(1,128)}, u32[]{:S(2)}) copy-start(f32[1,3072]{1,0:T(1,128)} %param.27) | copy-start | bytes 36868
  110.8 119.0 %collective-permute-start = (bf16[3,128,768]{2,1,0:T(8,128)(2,1)}, bf16[3,128,768]{2,1,0:T(8,128)(2,1)S(1)}, u32[]{:S(2)}, u32[]{:S(2)}) collective-permute-start(bf16[3,128,768]{2,1,0:T(8,128)(2,1)} %get-tuple-element.7), channel_id=1, source_target_pairs={{0,1},{1,2},{2,3},{3,0},{4,5},{5,6},{6,7},{7,4},{8,9},{9,10},{10,1... | collective-permute-start | bytes 1769480 | tf_op jit(solution)/shard_map/ppermute | solution.py:103
  110.8 119.0 %collective-permute-start.1 = (bf16[3,128,768]{2,1,0:T(8,128)(2,1)}, bf16[3,128,768]{2,1,0:T(8,128)(2,1)S(1)}, u32[]{:S(2)}, u32[]{:S(2)}) collective-permute-start(bf16[3,128,768]{2,1,0:T(8,128)(2,1)} %get-tuple-element.9), channel_id=1, source_target_pairs={{0,2},{1,3},{2,0},{3,1},{4,6},{5,7},{6,4},{7,5},{8,10},{9,11},{10,... | collective-permute-start | bytes 1769480 | tf_op jit(solution)/shard_map/ppermute | solution.py:103
  113.2 116.6 %collective-permute-start.2 = (bf16[3,128,768]{2,1,0:T(8,128)(2,1)}, bf16[3,128,768]{2,1,0:T(8,128)(2,1)}, u32[]{:S(2)}, u32[]{:S(2)}) collective-permute-start(bf16[3,128,768]{2,1,0:T(8,128)(2,1)} %get-tuple-element.6), channel_id=1, source_target_pairs={{0,3},{1,0},{2,1},{3,2},{4,7},{5,4},{6,5},{7,6},{8,11},{9,8},{10,9... | collective-permute-start | bytes 1769480 | tf_op jit(solution)/shard_map/ppermute | solution.py:103
  137.4 118.2 %collective-permute-start.6 = (bf16[128,64]{0,1:T(8,128)(2,1)S(1)}, bf16[128,64]{0,1:T(8,128)(2,1)S(1)}, u32[]{:S(2)}, u32[]{:S(2)}) collective-permute-start(bf16[128,64]{0,1:T(8,128)(2,1)S(1)} %fusion.22), channel_id=1, source_target_pairs={{0,1},{1,2},{2,3},{3,0},{4,5},{5,6},{6,7},{7,4},{8,9},{9,10},{10,1... | collective-permute-start | bytes 49160 | tf_op jit(solution)/shard_map/ppermute | solution.py:103
  139.0 119.5 %collective-permute-start.7 = (bf16[128,64]{0,1:T(8,128)(2,1)S(1)}, bf16[128,64]{0,1:T(8,128)(2,1)S(1)}, u32[]{:S(2)}, u32[]{:S(2)}) collective-permute-start(bf16[128,64]{0,1:T(8,128)(2,1)S(1)} %fusion.22), channel_id=1, source_target_pairs={{0,2},{1,3},{2,0},{3,1},{4,6},{5,7},{6,4},{7,5},{8,10},{9,11},{10,... | collective-permute-start | bytes 49160 | tf_op jit(solution)/shard_map/ppermute | solution.py:103
  242.8 78.5 %collective-permute-start.3 = (bf16[128,3072]{1,0:T(8,128)(2,1)}, bf16[128,3072]{1,0:T(8,128)(2,1)S(1)}, u32[]{:S(2)}, u32[]{:S(2)}) collective-permute-start(bf16[128,3072]{1,0:T(8,128)(2,1)} %convolution_convert_fusion.4), channel_id=1, source_target_pairs={{0,3},{1,0},{2,1},{3,2},{4,7},{5,4},{6,5},{7,6},{8,11},{9,8},{10,9... | collective-permute-start | bytes 2359304 | tf_op jit(solution)/shard_map/ppermute | solution.py:103
  250.2 71.2 %collective-permute-start.4 = (bf16[128,3072]{1,0:T(8,128)(2,1)}, bf16[128,3072]{1,0:T(8,128)(2,1)}, u32[]{:S(2)}, u32[]{:S(2)}) collective-permute-start(bf16[128,3072]{1,0:T(8,128)(2,1)} %convolution_convert_fusion.3), channel_id=1, source_target_pairs={{0,2},{1,3},{2,0},{3,1},{4,6},{5,7},{6,4},{7,5},{8,10},{9,11},{10,... | collective-permute-start | bytes 2359304 | tf_op jit(solution)/shard_map/ppermute | solution.py:103
  254.2 67.2 %collective-permute-start.5 = (bf16[128,3072]{1,0:T(8,128)(2,1)}, bf16[128,3072]{1,0:T(8,128)(2,1)}, u32[]{:S(2)}, u32[]{:S(2)}) collective-permute-start(bf16[128,3072]{1,0:T(8,128)(2,1)} %convolution_convert_fusion.2), channel_id=1, source_target_pairs={{0,1},{1,2},{2,3},{3,0},{4,5},{5,6},{6,7},{7,4},{8,9},{9,10},{10,1... | collective-permute-start | bytes 2359304 | tf_op jit(solution)/shard_map/ppermute | solution.py:103
  255.7 42.2 %collective-permute-start.8 = (bf16[128,64]{0,1:T(8,128)(2,1)S(1)}, bf16[128,64]{0,1:T(8,128)(2,1)S(1)}, u32[]{:S(2)}, u32[]{:S(2)}) collective-permute-start(bf16[128,64]{0,1:T(8,128)(2,1)S(1)} %fusion.22), channel_id=1, source_target_pairs={{0,3},{1,0},{2,1},{3,2},{4,7},{5,4},{6,5},{7,6},{8,11},{9,8},{10,9... | collective-permute-start | bytes 49160 | tf_op jit(solution)/shard_map/ppermute | solution.py:103
  258.4 57.6 %collective-permute-start.10 = (bf16[128,64]{0,1:T(8,128)(2,1)S(1)}, bf16[128,64]{0,1:T(8,128)(2,1)S(1)}, u32[]{:S(2)}, u32[]{:S(2)}) collective-permute-start(bf16[128,64]{0,1:T(8,128)(2,1)S(1)} %get-tuple-element.14), channel_id=1, source_target_pairs={{0,2},{1,3},{2,0},{3,1},{4,6},{5,7},{6,4},{7,5},{8,10},{9,11},{10,... | collective-permute-start | bytes 49160 | tf_op jit(solution)/shard_map/ppermute | solution.py:103
  297.9 22.7 %collective-permute-start.11 = (bf16[128,64]{0,1:T(8,128)(2,1)S(1)}, bf16[128,64]{0,1:T(8,128)(2,1)S(1)}, u32[]{:S(2)}, u32[]{:S(2)}) collective-permute-start(bf16[128,64]{0,1:T(8,128)(2,1)S(1)} %get-tuple-element.13), channel_id=1, source_target_pairs={{0,1},{1,2},{2,3},{3,0},{4,5},{5,6},{6,7},{7,4},{8,9},{9,10},{10,1... | collective-permute-start | bytes 49160 | tf_op jit(solution)/shard_map/ppermute | solution.py:103
  316.0 5.0 %collective-permute-start.9 = (bf16[128,64]{0,1:T(8,128)(2,1)S(1)}, bf16[128,64]{0,1:T(8,128)(2,1)S(1)}, u32[]{:S(2)}, u32[]{:S(2)}) collective-permute-start(bf16[128,64]{0,1:T(8,128)(2,1)S(1)} %get-tuple-element.12), channel_id=1, source_target_pairs={{0,3},{1,0},{2,1},{3,2},{4,7},{5,4},{6,5},{7,6},{8,11},{9,8},{10,9... | collective-permute-start | bytes 49160 | tf_op jit(solution)/shard_map/ppermute | solution.py:103
  320.5 87.8 %reduce-scatter.10.cloned.1.call-start = ((), (), s32[]{:S(2)}) async-start(), calls=%async_computation.10 | async-start | bytes 884736
  (12 other events, 140.7 us)
Sparse Core Ops, SparseCore 0:
  26.9 29.9 reduce-scatter.5
  83.2 23.3 reduce-scatter.7
Sparse Core Ops, SparseCore 1:
  29.1 49.1 all-gather.5
  97.6 38.4 all-gather.9
  137.8 25.4 all-gather.11
  165.2 58.5 all-gather.7
  320.6 48.7 all-reduce.1
  372.6 35.7 reduce-scatter.9

commit v2 on v1

--- a/solution.py
+++ b/solution.py
@@ -71,6 +71,231 @@
             transcendentals=heads * blocks * rows * (blocks * rows + text),
         ),
     )(length.reshape(1), text_gain.reshape(1, HD), image_gain, key_value, key_value, *image_blocks)
+
+
+def peers(axis):
+    size, rank = lax.axis_size(axis), lax.axis_index(axis)
+    return [(k, lax.rem(rank + k, size)) for k in range(1, size)]
+
+
+def greet(*axes):
+    barrier = pltpu.get_barrier_semaphore()
+    count = 0
+    for axis in axes:
+        for _, peer in peers(axis):
+            pl.semaphore_signal(
+                barrier, inc=1, device_id={axis: peer}, device_id_type=pl.DeviceIdType.MESH
+            )
+            count += 1
+    pl.semaphore_wait(barrier, count)
+
+
+def send(source, target, send_sem, recv_sem, axis, peer):
+    copy = pltpu.make_async_remote_copy(
+        src_ref=source,
+        dst_ref=target,
+        send_sem=send_sem,
+        recv_sem=recv_sem,
+        device_id={axis: peer},
+        device_id_type=pl.DeviceIdType.MESH,
+    )
+    copy.start()
+    return copy
+
+
+def finish(copies):
+    for copy in copies:
+        copy.wait()
+
+
+def sems(count):
+    return [pltpu.SemaphoreType.DMA((count,)), pltpu.SemaphoreType.DMA((count,))]
+
+
+VMEM = pl.BlockSpec(memory_space=pltpu.VMEM)
+SMEM = pl.BlockSpec(memory_space=pltpu.SMEM)
+
+
+def params(collective_id):
+    return pltpu.CompilerParams(
+        collective_id=collective_id, has_side_effects=True, vmem_limit_bytes=40 * 2**20
+    )
+
+
+def feature_sum_kernel(
+    part_ref, tokens_ref, gain_ref, squares_ref, encoded_ref, norm_ref, slots, square_slots, ss, sr, qs, qr
+):
+    width = tokens_ref.shape[1]
+    rank = lax.axis_index("seq")
+    greet("seq")
+    copies = []
+    for k, peer in peers("seq"):
+        copies.append(
+            send(squares_ref, square_slots.at[k - 1], qs.at[k - 1], qr.at[k - 1], "seq", peer)
+        )
+        columns = pl.ds(pl.multiple_of(peer * width, 128), width)
+        copies.append(
+            send(part_ref.at[:, columns], slots.at[k - 1], ss.at[k - 1], sr.at[k - 1], "seq", peer)
+        )
+    finish(copies)
+    own = pl.ds(pl.multiple_of(rank * width, 128), width)
+    total = part_ref[:, own].astype(jnp.float32)
+    squares = squares_ref[...]
+    for k, _ in peers("seq"):
+        total = total + slots[k - 1].astype(jnp.float32)
+        squares = squares + square_slots[k - 1]
+    encoded_ref[...] = ((tokens_ref[...].astype(jnp.float32) + total) * gain_ref[...]).astype(
+        encoded_ref.dtype
+    )
+    norm_ref[...] = jnp.sqrt(squares + EPSILON)
+
+
+def feature_sum(part, own_tokens, own_gain, squares):
+    others = lax.axis_size("seq") - 1
+    text, width = own_tokens.shape
+    return pl.pallas_call(
+        feature_sum_kernel,
+        out_shape=[
+            jax.ShapeDtypeStruct((text, width), jnp.bfloat16),
+            jax.ShapeDtypeStruct(squares.shape, jnp.float32),
+        ],
+        in_specs=[VMEM] * 4,
+        out_specs=[VMEM] * 2,
+        scratch_shapes=[
+            pltpu.VMEM((others, text, width), jnp.bfloat16),
+            pltpu.VMEM((others,) + squares.shape, jnp.float32),
+        ]
+        + sems(others)
+        + sems(others),
+        compiler_params=params(1),
+    )(part, own_tokens, own_gain, squares)
+
+
+def route_kernel(
+    owner_ref, part_ref, scale_ref, shift_ref, out_ref, slots, stage, prompts, final, ss, sr, ps, pr, fs, fr
+):
+    rows = stage.shape[0]
+    rank, data_rank = lax.axis_index("seq"), lax.axis_index("dp")
+    data_devices = lax.axis_size("dp")
+    greet("seq", "dp")
+
+    def block(index):
+        return pl.ds(pl.multiple_of(index * rows, 16), rows)
+
+    finish(
+        [
+            send(part_ref.at[block(peer)], slots.at[k - 1], ss.at[k - 1], sr.at[k - 1], "seq", peer)
+            for k, peer in peers("seq")
+        ]
+    )
+    total = part_ref[block(rank), :].astype(jnp.float32)
+    for k, _ in peers("seq"):
+        total = total + slots[k - 1].astype(jnp.float32)
+    stage[...] = total.astype(stage.dtype)
+    finish(
+        [
+            send(stage, prompts.at[k - 1], ps.at[k - 1], pr.at[k - 1], "dp", peer)
+            for k, peer in peers("dp")
+        ]
+    )
+    routed = jnp.where(owner_ref[data_rank] == data_rank, stage[...].astype(jnp.float32), 0.0)
+    for k, _ in peers("dp"):
+        prompt = lax.rem(data_rank + data_devices - k, data_devices)
+        routed = routed + jnp.where(
+            owner_ref[prompt] == data_rank, prompts[k - 1].astype(jnp.float32), 0.0
+        )
+    centre = jnp.mean(routed, -1, keepdims=True)
+    spread = jnp.mean((routed - centre) * (routed - centre), -1, keepdims=True)
+    layer_normed = (routed - centre) * lax.rsqrt(spread + EPSILON)
+    final[...] = ((1.0 + scale_ref[...]) * layer_normed + shift_ref[...]).astype(final.dtype)
+    copies = [
+        send(final, out_ref.at[block(rank)], fs.at[k - 1], fr.at[k - 1], "seq", peer)
+        for k, peer in peers("seq")
+    ]
+    out_ref[block(rank), :] = final[...]
+    finish(copies)
+
+
+def route(owner, part, scale, shift):
+    others, data_others = lax.axis_size("seq") - 1, lax.axis_size("dp") - 1
+    text, width = part.shape
+    rows = text // (others + 1)
+    return pl.pallas_call(
+        route_kernel,
+        out_shape=jax.ShapeDtypeStruct((text, width), jnp.bfloat16),
+        in_specs=[SMEM] + [VMEM] * 3,
+        out_specs=VMEM,
+        scratch_shapes=[
+            pltpu.VMEM((others, rows, width), jnp.bfloat16),
+            pltpu.VMEM((rows, width), jnp.bfloat16),
+            pltpu.VMEM((data_others, rows, width), jnp.bfloat16),
+            pltpu.VMEM((rows, width), jnp.bfloat16),
+        ]
+        + sems(others)
+        + sems(data_others)
+        + sems(others),
+        compiler_params=params(2),
+    )(owner, part, scale, shift)
+
+
+def gradient_sum_kernel(
+    cols_ref, down_ref, cols_out, down_out, cols_slots, down_slots, stage, stage_slots, down_stage, down_all,
+    cs, cr, ds, dr, ss, sr, gs, gr,
+):
+    data_rank = lax.axis_index("dp")
+    greet("seq", "dp")
+    copies = []
+    for k, peer in peers("dp"):
+        copies.append(send(cols_ref.at[peer], cols_slots.at[k - 1], cs.at[k - 1], cr.at[k - 1], "dp", peer))
+        copies.append(send(down_ref.at[peer], down_slots.at[k - 1], ds.at[k - 1], dr.at[k - 1], "dp", peer))
+    finish(copies)
+    cols = cols_ref[data_rank].astype(jnp.float32)
+    down = down_ref[data_rank].astype(jnp.float32)
+    for k, _ in peers("dp"):
+        cols = cols + cols_slots[k - 1].astype(jnp.float32)
+        down = down + down_slots[k - 1].astype(jnp.float32)
+    stage[...] = cols.astype(stage.dtype)
+    down_stage[...] = down.astype(down_stage.dtype)
+    copies = [
+        send(stage, stage_slots.at[k - 1], ss.at[k - 1], sr.at[k - 1], "seq", peer)
+        for k, peer in peers("seq")
+    ] + [
+        send(down_stage, down_all.at[data_rank], gs.at[k - 1], gr.at[k - 1], "dp", peer)
+        for k, peer in peers("dp")
+    ]
+    down_all[data_rank] = down_stage[...]
+    finish(copies)
+    cols = stage[...].astype(jnp.float32)
+    for k, _ in peers("seq"):
+        cols = cols + stage_slots[k - 1].astype(jnp.float32)
+    cols_out[...] = cols
+    down_out[...] = down_all[...].astype(jnp.float32)
+
+
+def gradient_sum(cols, down):
+    others, data_others = lax.axis_size("seq") - 1, lax.axis_size("dp") - 1
+    return pl.pallas_call(
+        gradient_sum_kernel,
+        out_shape=[
+            jax.ShapeDtypeStruct(cols.shape[1:], jnp.float32),
+            jax.ShapeDtypeStruct(down.shape, jnp.float32),
+        ],
+        in_specs=[VMEM] * 2,
+        out_specs=[VMEM] * 2,
+        scratch_shapes=[
+            pltpu.VMEM((data_others,) + cols.shape[1:], jnp.bfloat16),
+            pltpu.VMEM((data_others,) + down.shape[1:], jnp.bfloat16),
+            pltpu.VMEM(cols.shape[1:], jnp.bfloat16),
+            pltpu.VMEM((others,) + cols.shape[1:], jnp.bfloat16),
+            pltpu.VMEM(down.shape[1:], jnp.bfloat16),
+            pltpu.VMEM(down.shape, jnp.bfloat16),
+        ]
+        + sems(data_others)
+        + sems(data_others)
+        + sems(others)
+        + sems(data_others),
+        compiler_params=params(3),
+    )(cols, down)
 
 
 def on_device(
@@ -102,6 +327,10 @@
     def shifted(values, step):
         return lax.ppermute(values, "seq", [(i, (i + step) % seq_devices) for i in range(seq_devices)])
 
+    kv_own = kv_weight.reshape(kv_weight.shape[0], -1)
+    context_columns = lax.all_gather(context_weight, "dp", axis=1, tiled=True)
+    kv_rows = lax.all_gather(kv_own, "dp", axis=0, tiled=True)
+
     image_rows = jnp.transpose(image_query_key_value[0], (1, 0, 2))
     head_width = image_rows.shape[2] // seq_devices
 
@@ -113,48 +342,30 @@
     ]
 
     direction = proj_weight.astype(f32) + jnp.dot(dora_a, dora_b, precision=lax.Precision.HIGHEST)
-    column_norm = jnp.sqrt(lax.psum(jnp.sum(direction * direction, 0), "seq") + EPSILON)
-    ratio = magnitude / column_norm
-    gathered = lax.all_gather(
-        jnp.concatenate([(direction * ratio).astype(bf16), (dora_b * ratio).astype(bf16)], 0),
-        "dp",
-        axis=1,
-        tiled=True,
-    )
-    scaled, scaled_up = gathered[: dora_a.shape[0]], gathered[dora_a.shape[0] :]
+    squares = jnp.sum(direction * direction, 0, keepdims=True)
 
     tokens = enc_states[0, :MAX_PROMPT]
-    text_length, width_enc = tokens.shape
+    _, width_enc = tokens.shape
     feat_width = width_enc // seq_devices
-    own_tokens = lax.dynamic_slice_in_dim(tokens, seq_rank * feat_width, feat_width, 1).astype(f32)
+    own_tokens = lax.dynamic_slice_in_dim(tokens, seq_rank * feat_width, feat_width, 1)
     own_final = lax.dynamic_slice_in_dim(t5_final_gain, seq_rank * feat_width, feat_width, 0)
     normed = rms_scale(tokens.astype(f32), t5_gain).astype(bf16)
     gate_proj = jnp.dot(normed, t5_in_weight[0], preferred_element_type=f32)
     upward = jnp.dot(normed, t5_in_weight[1], preferred_element_type=f32)
     hidden = (jax.nn.gelu(gate_proj, approximate=True) * upward).astype(bf16)
-    ffn_part = lax.psum_scatter(
-        jnp.dot(hidden, t5_out_weight, preferred_element_type=f32).astype(bf16),
-        "seq",
-        scatter_dimension=1,
-        tiled=True,
-    ).astype(f32)
-    encoded = ((own_tokens + ffn_part) * own_final).astype(bf16)
-    context_part = jnp.dot(
-        encoded,
-        lax.all_gather(context_weight, "dp", axis=1, tiled=True),
-        preferred_element_type=f32,
-    )
-    text_tokens = lax.psum_scatter(context_part.astype(bf16), "seq", scatter_dimension=0, tiled=True)
-    routes = prompt_owner_sample == data_rank
-    diffusion_length = jnp.sum(jnp.where(routes, lengths, 0))
-    prompts = lax.all_gather(text_tokens[None], "dp", axis=0, tiled=True)
-    routed = jnp.sum(jnp.where(routes[:, None, None], prompts, jnp.zeros_like(prompts)), 0).astype(f32)
-    centre = jnp.mean(routed, -1, keepdims=True)
-    spread = jnp.mean((routed - centre) * (routed - centre), -1, keepdims=True)
-    layer_normed = (routed - centre) * lax.rsqrt(spread + EPSILON)
-    modulated = ((1.0 + text_scale) * layer_normed + text_shift).astype(bf16)
-    text_all = lax.all_gather(modulated, "seq", axis=0, tiled=True)
-    kv_rows = lax.all_gather(kv_weight.reshape(kv_weight.shape[0], -1), "dp", axis=0, tiled=True)
+    ffn_part = jnp.dot(hidden, t5_out_weight, preferred_element_type=f32).astype(bf16)
+    encoded, column_norm = feature_sum(ffn_part, own_tokens, own_final[None], squares)
+    context_part = jnp.dot(encoded, context_columns, preferred_element_type=f32).astype(bf16)
+    ratio = magnitude / column_norm[0]
+    own_scaled = jnp.concatenate(
+        [(direction * ratio).astype(bf16), (dora_b * ratio).astype(bf16)], 0
+    )
+    own_scaled, context_part = lax.optimization_barrier((own_scaled, context_part))
+    gathered = lax.all_gather(own_scaled, "dp", axis=1, tiled=True)
+    scaled, scaled_up = gathered[: dora_a.shape[0]], gathered[dora_a.shape[0] :]
+    diffusion_length = jnp.sum(jnp.where(prompt_owner_sample == data_rank, lengths, 0))
+    text_all = route(prompt_owner_sample, context_part, text_scale, text_shift)
+
     key_value = jnp.dot(text_all, kv_rows, preferred_element_type=f32)
 
     attended = attention(diffusion_length, text_key_gain, image_qk_gain, key_value, image_blocks)
@@ -175,21 +386,21 @@
         total, up_total = total + part.astype(f32), up_total + up_part.astype(f32)
     image_out = total.astype(bf16)
 
-    grad_a = lax.psum(
-        lax.dot_general(
-            attended, down_rows, (((0,), (0,)), ((), ())), preferred_element_type=f32
-        ).astype(bf16),
-        "dp",
-    ).astype(f32)
+    grad_down = lax.dot_general(
+        attended, down_rows, (((0,), (0,)), ((), ())), preferred_element_type=f32
+    ).astype(bf16)
     grad_up = lax.dot_general(
         up_total.astype(bf16), grad_out[0], (((0,), (0,)), ((), ())), preferred_element_type=f32
     )
     grad_size = jnp.sum(grad_out[0].astype(f32) * total, 0, keepdims=True)
-    column_parts = lax.psum_scatter(
-        jnp.concatenate([grad_up, grad_size], 0).astype(bf16), "dp", scatter_dimension=1, tiled=True
-    )
-    column_sums = lax.psum(column_parts, "seq").astype(f32)
-    rank = dora_b.shape[0]
+    rank, data_devices = dora_b.shape[0], lax.axis_size("dp")
+    spare = jnp.zeros((15, grad_size.shape[1]), f32)
+    columns = jnp.concatenate([grad_up, grad_size, spare], 0).astype(bf16)
+    columns = columns.reshape(rank + 16, data_devices, -1).transpose(1, 0, 2)
+    column_sums, grad_a = gradient_sum(
+        columns, grad_down.reshape(data_devices, -1, rank)
+    )
+    grad_a = grad_a.reshape(-1, rank)
     grad_b = column_sums[:rank] * ratio
     grad_magnitude = column_sums[rank] / magnitude
     return (image_out[None], grad_a, grad_b, grad_magnitude)

time: 438 us -> 309 us (0.71)
  waiting for transfers between devices: 259 us -> 54.3 us
  Pallas kernels: 7.85 us -> 147 us
  blocking collectives: 51.4 us -> 0 us
  matrix products: 49.1 us -> 43.2 us
    pallas_call x0 -> x3, Pallas kernels: none -> 139 us  [the longest x1 99.6 us: route(): pl.pallas_call(route_kernel, out_shape=jax.ShapeDtypeStruct((text, width)...]
    all_gather x4 -> x3, waiting for transfers between devices: 103 us -> 2.79 us  [the longest x1 2.75 us: on_device(): context_columns = lax.all_gather(context_weight, 'dp', axis=1, tiled=True)]
    psum x1 -> x0, waiting for transfers between devices: 41.8 us -> none  [on_device(): lax.psum(lax.dot_general(attended, down_rows, (((0,), (0,)), ((), ())), p...]
    reduce_scatter x2 -> x0, waiting for transfers between devices: 37.9 us -> none  [the longest x1 28.8 us: on_device(): lax.psum_scatter(jnp.dot(hidden, t5_out_weight, preferred_element_type=f3...]
    unnamed x9 -> x3, waiting for transfers between devices: 38 us -> 0.71 us
    psum x2 -> x0, blocking collectives: 31.6 us -> none  [the longest x1 19.6 us: on_device(): column_sums = lax.psum(column_parts, 'seq').astype(f32)]
    all_gather x1 -> x0, blocking collectives: 19.7 us -> none  [on_device(): text_all = lax.all_gather(modulated, 'seq', axis=0, tiled=True)]
    ppermute x12, waiting for transfers between devices: 38.8 us -> 50.8 us  [shifted(): lax.ppermute(values, 'seq', [(i, (i + step) % seq_devices) for i in range...]
  transfers between devices with their start and end apart: 20 -> 15, of which waited for: 10 -> 6; matrix products, arithmetic and copies ran while one was open for 9% -> 14% of each run, Pallas kernels for 2% -> 42%
where the time goes in v2:
time: 309 us
  Pallas kernels  147 us (48%)
  waiting for transfers between devices  54.3 us (18%)
  matrix products  43.2 us (14%)
  starting transfers between devices  37.7 us (12%)
  between operations  14.1 us (5%)
  local copies, waits for them, and re-layouts  8.3 us (3%)
  other arithmetic  4.61 us (1%)
    pallas_call x1, Pallas kernels, route(): pl.pallas_call(route_kernel, out_shape=jax.ShapeDtypeStruct((text, width)...  99.6 us
    ppermute x12, waiting for transfers between devices, shifted(): lax.ppermute(values, 'seq', [(i, (i + step) % seq_devices) for i in range...  50.8 us
    ppermute x12, starting transfers between devices, shifted(): lax.ppermute(values, 'seq', [(i, (i + step) % seq_devices) for i in range...  37.5 us
    pallas_call x1, Pallas kernels, feature_sum(): pl.pallas_call(feature_sum_kernel, out_shape=[jax.ShapeDtypeStruct((text,...  23.5 us
    pallas_call x1, Pallas kernels, gradient_sum(): pl.pallas_call(gradient_sum_kernel, out_shape=[jax.ShapeDtypeStruct(cols....  15.6 us
    dot_general x4, matrix products, on_device(): part = jnp.dot(block, scaled, preferred_element_type=f32).astype(bf16)  12.9 us
    dot_general x1, matrix products, on_device(): jnp.dot(hidden, t5_out_weight, preferred_element_type=f32).astype(bf16)  11.1 us
    pallas_call x1, Pallas kernels, attention(): pl.pallas_call(functools.partial(attention_kernel, blocks), grid=(heads,)...  7.93 us
  transfers between devices with their start and end apart: 15, of which 6 were waited for; matrix products, arithmetic and copies ran while one was open for 14% of the time, Pallas kernels for 42%

profile of v2, /device:TPU:0, one launch (start us, length us, event | category | flops | bytes accessed | tf_op | source)
XLA Modules:
  0.0 308.8 jit_solution(9045814832305665012)
XLA Ops:
  7.9 2.4 copy.31
  13.5 1.5 fusion.17
  15.1 5.6 %fusion.31 = f32[128,1280]{1,0:T(8,128)S(1)} fusion(bf16[2,4096,1280]{2,1,0:T(8,128)(2,1)} %param.23, f32[4096]{0:T(1024)S(1)} %copy-done.16, f32[128]{0:T(128)S(1)} %add_rsqrt_fusion, bf16[1,256,4096]{2,1,0:T(8,128)(2,1)} %param.19), kind=kOutput, calls=%fused_computation.44 | convolution fusion | flops 1345585152 | bytes 12206592 | tf_op jit(solution)/shard_map/dot_general | solution.py:353
  20.7 11.1 %convolution_convert_fusion.part_ref = bf16[128,4096]{1,0:T(8,128)(2,1)S(1)} fusion(bf16[1280,4096]{1,0:T(8,128)(2,1)} %param.24, f32[128,1280]{1,0:T(8,128)S(1)} %fusion.31, bf16[2,4096,1280]{2,1,0:T(8,128)(2,1)} %param.23, f32[4096]{0:T(1024)S(1)} %copy-done.17, f32[128]{0:T(128)S(1)} %add_rsqrt_fusion, bf16[1,256,4096]{2,1,0:T(8,128)(2,1)} %param.19), kind=kOutput, calls=%fused_computation.6 | convolution fusion | flops 2687303680 | bytes 23740928 | tf_op jit(solution)/shard_map/dot_general | solution.py:356
  31.8 23.5 %shard_map.210 = (bf16[128,1024]{1,0:T(8,128)(2,1)S(1)}, f32[1,384]{1,0:T(1,128)S(1)}) custom-call(bf16[128,4096]{1,0:T(8,128)(2,1)S(1)} %convolution_convert_fusion.part_ref, bf16[128,1024]{1,0:T(8,128)(2,1)S(1)} %dynamic-slice_bitcast_fusion.4.tokens_ref, f32[1,1024]{1,0:T(1,128)S(1)} %bitcast.72, f32[1,384]{1,0:T(1,128)S(1)} %broadcast_in_dim.24.squares_ref), custom_call_target="tpu_custom_call" | custom-call | tf_op jit(solution)/shard_map/pallas_call | solution.py:156
  56.4 2.8 all-gather.4.cloned.1.call-done
  59.2 3.9 %convolution_convert_fusion.5.part_ref = bf16[128,3072]{1,0:T(8,128)(2,1)S(1)} fusion(bf16[128,1024]{1,0:T(8,128)(2,1)S(1)} %get-tuple-element.11, bf16[1024,3072]{1,0:T(8,128)(2,1)} %all-gather.4.cloned.1.call-done), kind=kOutput, calls=%fused_computation.12 | convolution fusion | flops 805699584 | bytes 7340032 | tf_op jit(solution)/shard_map/dot_general | solution.py:358
  63.2 1.5 dynamic-slice_bitcast_fusion
  64.7 3.4 %collective-permute-start = (bf16[3,128,768]{2,1,0:T(8,128)(2,1)}, bf16[3,128,768]{2,1,0:T(8,128)(2,1)S(1)}, u32[]{:S(2)}, u32[]{:S(2)}) collective-permute-start(bf16[3,128,768]{2,1,0:T(8,128)(2,1)} %get-tuple-element.25), channel_id=1, source_target_pairs={{0,1},{1,2},{2,3},{3,0},{4,5},{5,6},{6,7},{7,4},{8,9},{9,10},{10,1... | collective-permute-start | bytes 1769480 | tf_op jit(solution)/shard_map/ppermute | solution.py:328
  68.1 2.5 collective-permute-start.1
  71.2 99.6 %shard_map.211 = bf16[128,3072]{1,0:T(8,128)(2,1)S(1)} custom-call(s32[8]{0:T(128)S(1)} %copy-done.2, bf16[128,3072]{1,0:T(8,128)(2,1)S(1)} %convolution_convert_fusion.5.part_ref, f32[1,3072]{1,0:T(1,128)S(1)} %copy-done, f32[1,3072]{1,0:T(1,128)S(1)} %copy-done.1), custom_call_target="tpu_custom_call" | custom-call | tf_op jit(solution)/shard_map/pallas_call | solution.py:223
  170.9 6.0 %fusion.67.text_key_ref.text_value_ref = f32[128,1536]{1,0:T(8,128)} fusion(bf16[128,3072]{1,0:T(8,128)(2,1)S(1)} %shard_map.211, bf16[3072,1536]{1,0:T(8,128)(2,1)} %all-gather.6.cloned.1.call-done), kind=kOutput, calls=%fused_computation.78 | convolution fusion | flops 1207959552 | bytes 11010048 | tf_op jit(solution)/shard_map/dot_general | solution.py:369
  177.8 7.9 %shard_map.212 = bf16[512,768]{1,0:T(8,128)(2,1)} custom-call(s32[1]{0:T(128)} %bitcast.length_ref, f32[1,128]{1,0:T(1,128)} %bitcast.77, f32[2,128]{1,0:T(2,128)} %image_gain_ref.1, f32[128,1536]{1,0:T(8,128)} %fusion.67.text_key_ref.text_value_ref, f32[128,1536]{1,0:T(8,128)} %fusion.67.text_key_ref.text_value_ref, ...), custom_call_target="tpu_custom_call" | custom-call | flops 1006632960 | bytes 3145728 | tf_op jit(solution)/shard_map/pallas_call | solution.py:55
  187.3 4.3 %convolution_convert_fusion.4 = bf16[128,3072]{1,0:T(8,128)(2,1)} fusion(bf16[832,3072]{1,0:T(8,128)(2,1)} %all-gather.8.cloned.1.call-done, bf16[512,768]{1,0:T(8,128)(2,1)} %shard_map.212), kind=kOutput, calls=%fused_computation.11 | convolution fusion | flops 604372992 | bytes 5701632 | tf_op jit(solution)/shard_map/dot_general | solution.py:382
  191.6 5.3 %collective-permute-start.3 = (bf16[128,3072]{1,0:T(8,128)(2,1)}, bf16[128,3072]{1,0:T(8,128)(2,1)}, u32[]{:S(2)}, u32[]{:S(2)}) collective-permute-start(bf16[128,3072]{1,0:T(8,128)(2,1)} %convolution_convert_fusion.4), channel_id=1, source_target_pairs={{0,3},{1,0},{2,1},{3,2},{4,7},{5,4},{6,5},{7,6},{8,11},{9,8},{10,9... | collective-permute-start | bytes 2359304 | tf_op jit(solution)/shard_map/ppermute | solution.py:328
  196.9 1.7 convolution_convert_fusion.3
  199.5 1.7 convolution_convert_fusion.2
  201.3 3.9 %collective-permute-start.6 = (bf16[128,64]{0,1:T(8,128)(2,1)S(1)}, bf16[128,64]{0,1:T(8,128)(2,1)S(1)}, u32[]{:S(2)}, u32[]{:S(2)}) collective-permute-start(bf16[128,64]{0,1:T(8,128)(2,1)S(1)} %get-tuple-element.30), channel_id=1, source_target_pairs={{0,3},{1,0},{2,1},{3,2},{4,7},{5,4},{6,5},{7,6},{8,11},{9,8},{10,9... | collective-permute-start | bytes 49160 | tf_op jit(solution)/shard_map/ppermute | solution.py:328
  205.7 42.9 %collective-permute-done.6 = bf16[128,64]{0,1:T(8,128)(2,1)S(1)} collective-permute-done((bf16[128,64]{0,1:T(8,128)(2,1)S(1)}, bf16[128,64]{0,1:T(8,128)(2,1)S(1)}, u32[]{:S(2)}, u32[]{:S(2)}) %collective-permute-start.6) | collective-permute-done | bytes 16416 | tf_op jit(solution)/shard_map/ppermute | solution.py:328
  248.6 19.9 %collective-permute-start.8 = (bf16[128,64]{0,1:T(8,128)(2,1)S(1)}, bf16[128,64]{0,1:T(8,128)(2,1)S(1)}, u32[]{:S(2)}, u32[]{:S(2)}) collective-permute-start(bf16[128,64]{0,1:T(8,128)(2,1)S(1)} %get-tuple-element.31), channel_id=1, source_target_pairs={{0,1},{1,2},{2,3},{3,0},{4,5},{5,6},{6,7},{7,4},{8,9},{9,10},{10,1... | collective-permute-start | bytes 49160 | tf_op jit(solution)/shard_map/ppermute | solution.py:328
  271.5 1.8 collective-permute-done.10
  274.0 4.7 %collective-permute-done.9 = bf16[128,64]{0,1:T(8,128)(2,1)S(1)} collective-permute-done((bf16[128,64]{0,1:T(8,128)(2,1)S(1)}, bf16[128,64]{0,1:T(8,128)(2,1)S(1)}, u32[]{:S(2)}, u32[]{:S(2)}) %collective-permute-start.9) | collective-permute-done | bytes 16416 | tf_op jit(solution)/shard_map/ppermute | solution.py:328
  279.2 5.2 %multiply_reduce_fusion = (bf16[3072]{0:T(1024)(128)(2,1)S(1)}, bf16[1,128,3072]{2,1,0:T(8,128)(2,1)}) fusion(bf16[1,128,3072]{2,1,0:T(8,128)(2,1)S(1)} %copy-done.4, bf16[832,3072]{1,0:T(8,128)(2,1)} %all-gather.8.cloned.1.call-done, bf16[512,768]{1,0:T(8,128)(2,1)S(1)} %copy-done.3, bf16[128,3072]{1,0:T(8,128)(2,1)} %collective-permute-done.5, ...), kind=kOutput, calls=%fused_computation.24 | convolution fusion | flops 608695296 | bytes 8853504 | tf_op jit(solution)/shard_map/dot_general | solution.py:382
  284.6 15.6 %shard_map.213 = (f32[80,384]{1,0:T(8,128)S(1)}, f32[8,96,64]{2,1,0:T(8,128)S(1)}) custom-call(bf16[8,80,384]{2,1,0:T(8,128)(2,1)S(1)} %maximum_bitcast_fusion.cols_ref, bf16[8,96,64]{2,1,0:T(8,128)(2,1)S(1)} %bitcast.70), custom_call_target="tpu_custom_call" | custom-call | tf_op jit(solution)/shard_map/pallas_call | solution.py:277
  (88 shorter events, 16.1 us)
Async XLA Ops:
  7.2 52.0 %all-gather.4.cloned.1.call-start = ((), (), s32[]{:S(2)}) async-start(), calls=%async_computation | async-start | bytes 7077888 | tf_op jit(solution)/shard_map/all_gather | solution.py:331
  7.9 162.9 %all-gather.6.cloned.1.call-start = ((), (), s32[]{:S(2)}) async-start(), calls=%async_computation.1 | async-start | bytes 10616832 | tf_op jit(solution)/shard_map/all_gather | solution.py:332
  10.4 176.9 %all-gather.8.cloned.1.call-start = ((), (), s32[]{:S(2)}) async-start(), calls=%async_computation.2 | async-start | bytes 5750784 | tf_op jit(solution)/shard_map/all_gather | solution.py:364
  20.7 34.7 %copy-start.14 = (f32[384]{0:T(512)S(1)}, f32[384]{0:T(512)}, u32[]{:S(2)}) copy-start(f32[384]{0:T(512)} %param.36) | copy-start | bytes 4612
  20.7 34.7 %copy-start.12 = (f32[64,384]{1,0:T(8,128)S(1)}, f32[64,384]{1,0:T(8,128)}, u32[]{:S(2)}) copy-start(f32[64,384]{1,0:T(8,128)} %param.35) | copy-start | bytes 294916
  63.2 7.4 %copy-start.2 = (s32[8]{0:T(128)S(1)}, s32[8]{0:T(128)}, u32[]{:S(2)}) copy-start(s32[8]{0:T(128)} %owner_ref.1) | copy-start | bytes 100
  63.2 7.4 %copy-start.15 = (s32[8]{0:T(128)S(1)}, s32[8]{0:T(128)}, u32[]{:S(2)}) copy-start(s32[8]{0:T(128)} %param.20) | copy-start | bytes 100
  63.2 8.0 %copy-start = (f32[1,3072]{1,0:T(1,128)S(1)}, f32[1,3072]{1,0:T(1,128)}, u32[]{:S(2)}) copy-start(f32[1,3072]{1,0:T(1,128)} %scale_ref.1) | copy-start | bytes 36868
  63.2 8.0 %copy-start.1 = (f32[1,3072]{1,0:T(1,128)S(1)}, f32[1,3072]{1,0:T(1,128)}, u32[]{:S(2)}) copy-start(f32[1,3072]{1,0:T(1,128)} %shift_ref.1) | copy-start | bytes 36868
  64.7 112.1 %collective-permute-start = (bf16[3,128,768]{2,1,0:T(8,128)(2,1)}, bf16[3,128,768]{2,1,0:T(8,128)(2,1)S(1)}, u32[]{:S(2)}, u32[]{:S(2)}) collective-permute-start(bf16[3,128,768]{2,1,0:T(8,128)(2,1)} %get-tuple-element.25), channel_id=1, source_target_pairs={{0,1},{1,2},{2,3},{3,0},{4,5},{5,6},{6,7},{7,4},{8,9},{9,10},{10,1... | collective-permute-start | bytes 1769480 | tf_op jit(solution)/shard_map/ppermute | solution.py:328
  68.1 108.7 %collective-permute-start.1 = (bf16[3,128,768]{2,1,0:T(8,128)(2,1)}, bf16[3,128,768]{2,1,0:T(8,128)(2,1)S(1)}, u32[]{:S(2)}, u32[]{:S(2)}) collective-permute-start(bf16[3,128,768]{2,1,0:T(8,128)(2,1)} %get-tuple-element.27), channel_id=1, source_target_pairs={{0,2},{1,3},{2,0},{3,1},{4,6},{5,7},{6,4},{7,5},{8,10},{9,11},{10,... | collective-permute-start | bytes 1769480 | tf_op jit(solution)/shard_map/ppermute | solution.py:328
  70.6 106.3 %collective-permute-start.2 = (bf16[3,128,768]{2,1,0:T(8,128)(2,1)}, bf16[3,128,768]{2,1,0:T(8,128)(2,1)}, u32[]{:S(2)}, u32[]{:S(2)}) collective-permute-start(bf16[3,128,768]{2,1,0:T(8,128)(2,1)} %get-tuple-element.24), channel_id=1, source_target_pairs={{0,3},{1,0},{2,1},{3,2},{4,7},{5,4},{6,5},{7,6},{8,11},{9,8},{10,9... | collective-permute-start | bytes 1769480 | tf_op jit(solution)/shard_map/ppermute | solution.py:328
  177.8 7.9 %copy-start.7 = (f32[768,64]{0,1:T(8,128)S(1)}, f32[768,64]{0,1:T(8,128)}, u32[]{:S(2)}) copy-start(f32[768,64]{0,1:T(8,128)} %param.34) | copy-start | bytes 589828
  187.3 9.6 %copy-start.3 = (bf16[512,768]{1,0:T(8,128)(2,1)S(1)}, bf16[512,768]{1,0:T(8,128)(2,1)}, u32[]{:S(2)}) copy-start(bf16[512,768]{1,0:T(8,128)(2,1)} %shard_map.212) | copy-start | bytes 2359300
  187.3 9.6 %copy-start.13 = (bf16[832,3072]{1,0:T(8,128)(2,1)S(1)}, bf16[832,3072]{1,0:T(8,128)(2,1)}, u32[]{:S(2)}) copy-start(bf16[832,3072]{1,0:T(8,128)(2,1)} %all-gather.8.cloned.1.call-done) | copy-start | bytes 15335428
  191.6 87.6 %collective-permute-start.3 = (bf16[128,3072]{1,0:T(8,128)(2,1)}, bf16[128,3072]{1,0:T(8,128)(2,1)}, u32[]{:S(2)}, u32[]{:S(2)}) collective-permute-start(bf16[128,3072]{1,0:T(8,128)(2,1)} %convolution_convert_fusion.4), channel_id=1, source_target_pairs={{0,3},{1,0},{2,1},{3,2},{4,7},{5,4},{6,5},{7,6},{8,11},{9,8},{10,9... | collective-permute-start | bytes 2359304 | tf_op jit(solution)/shard_map/ppermute | solution.py:328
  198.6 80.6 %collective-permute-start.4 = (bf16[128,3072]{1,0:T(8,128)(2,1)}, bf16[128,3072]{1,0:T(8,128)(2,1)}, u32[]{:S(2)}, u32[]{:S(2)}) collective-permute-start(bf16[128,3072]{1,0:T(8,128)(2,1)} %convolution_convert_fusion.3), channel_id=1, source_target_pairs={{0,2},{1,3},{2,0},{3,1},{4,6},{5,7},{6,4},{7,5},{8,10},{9,11},{10,... | collective-permute-start | bytes 2359304 | tf_op jit(solution)/shard_map/ppermute | solution.py:328
  201.2 78.0 %collective-permute-start.5 = (bf16[128,3072]{1,0:T(8,128)(2,1)}, bf16[128,3072]{1,0:T(8,128)(2,1)}, u32[]{:S(2)}, u32[]{:S(2)}) collective-permute-start(bf16[128,3072]{1,0:T(8,128)(2,1)} %convolution_convert_fusion.2), channel_id=1, source_target_pairs={{0,1},{1,2},{2,3},{3,0},{4,5},{5,6},{6,7},{7,4},{8,9},{9,10},{10,1... | collective-permute-start | bytes 2359304 | tf_op jit(solution)/shard_map/ppermute | solution.py:328
  201.3 47.4 %collective-permute-start.6 = (bf16[128,64]{0,1:T(8,128)(2,1)S(1)}, bf16[128,64]{0,1:T(8,128)(2,1)S(1)}, u32[]{:S(2)}, u32[]{:S(2)}) collective-permute-start(bf16[128,64]{0,1:T(8,128)(2,1)S(1)} %get-tuple-element.30), channel_id=1, source_target_pairs={{0,3},{1,0},{2,1},{3,2},{4,7},{5,4},{6,5},{7,6},{8,11},{9,8},{10,9... | collective-permute-start | bytes 49160 | tf_op jit(solution)/shard_map/ppermute | solution.py:328
  205.1 63.4 %collective-permute-start.7 = (bf16[128,64]{0,1:T(8,128)(2,1)S(1)}, bf16[128,64]{0,1:T(8,128)(2,1)S(1)}, u32[]{:S(2)}, u32[]{:S(2)}) collective-permute-start(bf16[128,64]{0,1:T(8,128)(2,1)S(1)} %get-tuple-element.32), channel_id=1, source_target_pairs={{0,2},{1,3},{2,0},{3,1},{4,6},{5,7},{6,4},{7,5},{8,10},{9,11},{10,... | collective-permute-start | bytes 49160 | tf_op jit(solution)/shard_map/ppermute | solution.py:328
  248.6 21.4 %collective-permute-start.8 = (bf16[128,64]{0,1:T(8,128)(2,1)S(1)}, bf16[128,64]{0,1:T(8,128)(2,1)S(1)}, u32[]{:S(2)}, u32[]{:S(2)}) collective-permute-start(bf16[128,64]{0,1:T(8,128)(2,1)S(1)} %get-tuple-element.31), channel_id=1, source_target_pairs={{0,1},{1,2},{2,3},{3,0},{4,5},{5,6},{6,7},{7,4},{8,9},{9,10},{10,1... | collective-permute-start | bytes 49160 | tf_op jit(solution)/shard_map/ppermute | solution.py:328
  268.6 4.6 %collective-permute-start.10 = (bf16[128,64]{0,1:T(8,128)(2,1)S(1)}, bf16[128,64]{0,1:T(8,128)(2,1)S(1)}, u32[]{:S(2)}, u32[]{:S(2)}) collective-permute-start(bf16[128,64]{0,1:T(8,128)(2,1)S(1)} %fusion.22), channel_id=1, source_target_pairs={{0,2},{1,3},{2,0},{3,1},{4,6},{5,7},{6,4},{7,5},{8,10},{9,11},{10,... | collective-permute-start | bytes 49160 | tf_op jit(solution)/shard_map/ppermute | solution.py:328
  270.0 4.0 %collective-permute-start.11 = (bf16[128,64]{0,1:T(8,128)(2,1)S(1)}, bf16[128,64]{0,1:T(8,128)(2,1)S(1)}, u32[]{:S(2)}, u32[]{:S(2)}) collective-permute-start(bf16[128,64]{0,1:T(8,128)(2,1)S(1)} %fusion.22), channel_id=1, source_target_pairs={{0,3},{1,0},{2,1},{3,2},{4,7},{5,4},{6,5},{7,6},{8,11},{9,8},{10,9... | collective-permute-start | bytes 49160 | tf_op jit(solution)/shard_map/ppermute | solution.py:328
  273.2 5.5 %collective-permute-start.9 = (bf16[128,64]{0,1:T(8,128)(2,1)S(1)}, bf16[128,64]{0,1:T(8,128)(2,1)S(1)}, u32[]{:S(2)}, u32[]{:S(2)}) collective-permute-start(bf16[128,64]{0,1:T(8,128)(2,1)S(1)} %fusion.22), channel_id=1, source_target_pairs={{0,1},{1,2},{2,3},{3,0},{4,5},{5,6},{6,7},{7,4},{8,9},{9,10},{10,1... | collective-permute-start | bytes 49160 | tf_op jit(solution)/shard_map/ppermute | solution.py:328
  (10 other events, 28.0 us)
Sparse Core Ops, SparseCore 0:
  9.8 49.2 all-gather.3
  61.1 58.6 all-gather.5
  121.7 50.7 all-gather.7

commit v3 on v2

--- a/solution.py
+++ b/solution.py
@@ -238,64 +238,234 @@
     )(owner, part, scale, shift)
 
 
-def gradient_sum_kernel(
-    cols_ref, down_ref, cols_out, down_out, cols_slots, down_slots, stage, stage_slots, down_stage, down_all,
-    cs, cr, ds, dr, ss, sr, gs, gr,
+def finish_kernel(
+    att_ref, weight_ref, dora_ref, down_ref, grad_ref, grad_blocks_ref,
+    image_out, size_out, cols_out, down_out,
+    parts, stage_r, stage_l, got_r, got_l, up, up_slots, down_slots,
+    cols, col_slots, col_stage, col_sums, rows_all, row_slots, row_stage, row_sums,
+    size, size_slots, size_stage, size_sums,
+    r_s, r_r, l_s, l_r, us, ur, ws, wr, cs, cr, c2s, c2r, as_, ar, a2s, a2r, gs, gr, g2s, g2r,
 ):
-    data_rank = lax.axis_index("dp")
+    count = lax.axis_size("seq")
+    rank, data_rank = lax.axis_index("seq"), lax.axis_index("dp")
+    rows, width = image_out.shape
+    depth = att_ref.shape[1]
+    half = width // 2
+    f32, bf16 = jnp.float32, jnp.bfloat16
+    over_rows = (((0,), (0,)), ((), ()))
+
+    def product(k):
+        block = att_ref[k * rows : (k + 1) * rows, :]
+        for h in range(2):
+            columns = slice(h * half, (h + 1) * half)
+            parts[k, h] = jnp.dot(block, weight_ref[:depth, columns], preferred_element_type=f32).astype(bf16)
+
+    def link(right, t, h):
+        stage, got, ss, rs = (stage_r, got_r, r_s, r_r) if right else (stage_l, got_l, l_s, l_r)
+        target = lax.rem(rank + (1 if right else count - 1), count)
+        return pltpu.make_async_remote_copy(
+            src_ref=stage.at[t - 1, h],
+            dst_ref=got.at[t - 1, h],
+            send_sem=ss.at[t - 1, h],
+            recv_sem=rs.at[t - 1, h],
+            device_id={"seq": target},
+            device_id_type=pl.DeviceIdType.MESH,
+        )
+
+    def chain(t, h):
+        for right in (True, False):
+            stage, got = (stage_r, got_r) if right else (stage_l, got_l)
+            place = rank if right else count - 1 - rank
+            part = t if right else count - t
+
+            if t == 1:
+
+                @pl.when(place == 0)
+                def _():
+                    stage[0, h] = parts[part, h]
+                    link(right, 1, h).start()
+
+            else:
+
+                @pl.when(place == 0)
+                def _():
+                    stage[t - 1, h] = parts[part, h]
+                    link(right, t, h).start()
+
+                @pl.when((place >= 1) & (place <= t - 1))
+                def _():
+                    link(right, t - 1, h).wait_recv()
+                    stage[t - 1, h] = (
+                        parts[part, h].astype(f32) + got[t - 2, h].astype(f32)
+                    ).astype(bf16)
+                    link(right, t, h).start()
+
     greet("seq", "dp")
-    copies = []
+    done = {0}
+    for k in (1, count - 1):
+        if k not in done:
+            product(k)
+            done.add(k)
+    for h in range(2):
+        chain(1, h)
+
+    ups = jnp.dot(att_ref[...], dora_ref[...], preferred_element_type=f32).astype(bf16)
+    for k in range(count):
+        up[k] = ups[k * rows : (k + 1) * rows]
+    small = []
+    for k in range(1, count):
+        before = lax.rem(rank + count - k, count)
+        small.append(send(up.at[k], up_slots.at[k - 1], us.at[k - 1], ur.at[k - 1], "seq", before))
+        after = lax.rem(rank + k, count)
+        small.append(send(down_ref, down_slots.at[k - 1], ws.at[k - 1], wr.at[k - 1], "seq", after))
+    for t in range(2, count):
+        for k in (t, count - t):
+            if k not in done:
+                product(k)
+                done.add(k)
+    product(0)
+    finish(small)
+    up_total = up[0].astype(f32)
+    for k in range(1, count):
+        up_total = up_total + up_slots[k - 1].astype(f32)
+    up_total = up_total.astype(bf16)
+    blocks, block_rows = rows_all.shape[0], rows_all.shape[1]
+    for j in range(blocks):
+        cols[j] = lax.dot_general(
+            up_total, grad_blocks_ref[j], over_rows, preferred_element_type=f32
+        ).astype(bf16)
+    grad_rows = lax.dot_general(att_ref[:rows, :], down_ref[...], over_rows, preferred_element_type=f32)
+    for k in range(1, count):
+        grad_rows = grad_rows + lax.dot_general(
+            att_ref[k * rows : (k + 1) * rows, :], down_slots[k - 1], over_rows, preferred_element_type=f32
+        )
+    for j in range(blocks):
+        rows_all[j] = grad_rows[j * block_rows : (j + 1) * block_rows].astype(bf16)
+    first = []
     for k, peer in peers("dp"):
-        copies.append(send(cols_ref.at[peer], cols_slots.at[k - 1], cs.at[k - 1], cr.at[k - 1], "dp", peer))
-        copies.append(send(down_ref.at[peer], down_slots.at[k - 1], ds.at[k - 1], dr.at[k - 1], "dp", peer))
-    finish(copies)
-    cols = cols_ref[data_rank].astype(jnp.float32)
-    down = down_ref[data_rank].astype(jnp.float32)
+        first.append(send(cols.at[peer], col_slots.at[k - 1], cs.at[k - 1], cr.at[k - 1], "dp", peer))
+        first.append(send(rows_all.at[peer], row_slots.at[k - 1], as_.at[k - 1], ar.at[k - 1], "dp", peer))
+    second = []
+    for t in range(2, count):
+        for h in range(2):
+            chain(t, h)
+        if t == 2:
+            finish(first)
+            col_total = cols[data_rank].astype(f32)
+            row_total = rows_all[data_rank].astype(f32)
+            for k, _ in peers("dp"):
+                col_total = col_total + col_slots[k - 1].astype(f32)
+                row_total = row_total + row_slots[k - 1].astype(f32)
+            col_stage[...] = col_total.astype(bf16)
+            row_stage[...] = row_total.astype(bf16)
+            for k, peer in peers("seq"):
+                second.append(send(col_stage, col_sums.at[k - 1], c2s.at[k - 1], c2r.at[k - 1], "seq", peer))
+            for k, peer in peers("dp"):
+                second.append(
+                    send(row_stage, row_sums.at[data_rank], a2s.at[k - 1], a2r.at[k - 1], "dp", peer)
+                )
+            row_sums[data_rank] = row_stage[...]
+
+    for h in range(2):
+
+        @pl.when(rank >= 1)
+        def _():
+            link(True, count - 1, h).wait_recv()
+
+        @pl.when(rank <= count - 2)
+        def _():
+            link(False, count - 1, h).wait_recv()
+
+        columns = slice(h * half, (h + 1) * half)
+        total = parts[0, h].astype(f32)
+        total = total + jnp.where(rank >= 1, got_r[count - 2, h].astype(f32), 0.0)
+        total = total + jnp.where(rank <= count - 2, got_l[count - 2, h].astype(f32), 0.0)
+        image_out[:, columns] = total.astype(bf16)
+        size[:, columns] = jnp.sum(grad_ref[:, columns].astype(f32) * total, 0, keepdims=True)
+    last = [
+        send(size, size_slots.at[k - 1], gs.at[k - 1], gr.at[k - 1], "dp", peer) for k, peer in peers("dp")
+    ]
+    finish(second)
+    col_total = col_stage[...].astype(f32)
+    for k, _ in peers("seq"):
+        col_total = col_total + col_sums[k - 1].astype(f32)
+    cols_out[...] = col_total
+    down_out[...] = row_sums[...].astype(f32)
+    finish(last)
+    size_total = size[...]
     for k, _ in peers("dp"):
-        cols = cols + cols_slots[k - 1].astype(jnp.float32)
-        down = down + down_slots[k - 1].astype(jnp.float32)
-    stage[...] = cols.astype(stage.dtype)
-    down_stage[...] = down.astype(down_stage.dtype)
-    copies = [
-        send(stage, stage_slots.at[k - 1], ss.at[k - 1], sr.at[k - 1], "seq", peer)
-        for k, peer in peers("seq")
-    ] + [
-        send(down_stage, down_all.at[data_rank], gs.at[k - 1], gr.at[k - 1], "dp", peer)
-        for k, peer in peers("dp")
-    ]
-    down_all[data_rank] = down_stage[...]
-    finish(copies)
-    cols = stage[...].astype(jnp.float32)
+        size_total = size_total + size_slots[k - 1]
+    size_stage[...] = size_total
+    finish(
+        [
+            send(size_stage, size_sums.at[k - 1], g2s.at[k - 1], g2r.at[k - 1], "seq", peer)
+            for k, peer in peers("seq")
+        ]
+    )
     for k, _ in peers("seq"):
-        cols = cols + stage_slots[k - 1].astype(jnp.float32)
-    cols_out[...] = cols
-    down_out[...] = down_all[...].astype(jnp.float32)
-
-
-def gradient_sum(cols, down):
-    others, data_others = lax.axis_size("seq") - 1, lax.axis_size("dp") - 1
+        size_total = size_total + size_sums[k - 1]
+    size_out[...] = size_total
+    for t in range(1, count):
+        for h in range(2):
+
+            @pl.when(rank <= t - 1)
+            def _():
+                link(True, t, h).wait_send()
+
+            @pl.when(count - 1 - rank <= t - 1)
+            def _():
+                link(False, t, h).wait_send()
+
+
+def finish_step(attended, gathered, dora, down, grad, grad_blocks):
+    count, data_devices = lax.axis_size("seq"), lax.axis_size("dp")
+    depth, (rows, width) = attended.shape[1], grad.shape
+    rank, own_cols = down.shape[1], grad_blocks.shape[2]
+    block_rows = depth // data_devices
+    f32, bf16 = jnp.float32, jnp.bfloat16
+    halves = (rows, width // 2)
     return pl.pallas_call(
-        gradient_sum_kernel,
+        finish_kernel,
         out_shape=[
-            jax.ShapeDtypeStruct(cols.shape[1:], jnp.float32),
-            jax.ShapeDtypeStruct(down.shape, jnp.float32),
+            jax.ShapeDtypeStruct((rows, width), bf16),
+            jax.ShapeDtypeStruct((1, width), f32),
+            jax.ShapeDtypeStruct((rank, own_cols), f32),
+            jax.ShapeDtypeStruct((data_devices, block_rows, rank), f32),
         ],
-        in_specs=[VMEM] * 2,
-        out_specs=[VMEM] * 2,
+        in_specs=[VMEM] * 6,
+        out_specs=[VMEM] * 4,
         scratch_shapes=[
-            pltpu.VMEM((data_others,) + cols.shape[1:], jnp.bfloat16),
-            pltpu.VMEM((data_others,) + down.shape[1:], jnp.bfloat16),
-            pltpu.VMEM(cols.shape[1:], jnp.bfloat16),
-            pltpu.VMEM((others,) + cols.shape[1:], jnp.bfloat16),
-            pltpu.VMEM(down.shape[1:], jnp.bfloat16),
-            pltpu.VMEM(down.shape, jnp.bfloat16),
-        ]
-        + sems(data_others)
-        + sems(data_others)
-        + sems(others)
-        + sems(data_others),
-        compiler_params=params(3),
-    )(cols, down)
+            pltpu.VMEM((count, 2) + halves, bf16),
+        ]
+        + [pltpu.VMEM((count - 1, 2) + halves, bf16)] * 4
+        + [
+            pltpu.VMEM((count, rows, rank), bf16),
+            pltpu.VMEM((count - 1, rows, rank), bf16),
+            pltpu.VMEM((count - 1, rows, rank), bf16),
+            pltpu.VMEM((data_devices, rank, own_cols), bf16),
+            pltpu.VMEM((data_devices - 1, rank, own_cols), bf16),
+            pltpu.VMEM((rank, own_cols), bf16),
+            pltpu.VMEM((count - 1, rank, own_cols), bf16),
+            pltpu.VMEM((data_devices, block_rows, rank), bf16),
+            pltpu.VMEM((data_devices - 1, block_rows, rank), bf16),
+            pltpu.VMEM((block_rows, rank), bf16),
+            pltpu.VMEM((data_devices, block_rows, rank), bf16),
+            pltpu.VMEM((1, width), f32),
+            pltpu.VMEM((data_devices - 1, 1, width), f32),
+            pltpu.VMEM((1, width), f32),
+            pltpu.VMEM((count - 1, 1, width), f32),
+        ]
+        + [pltpu.SemaphoreType.DMA((count - 1, 2))] * 4
+        + sems(count - 1) * 2
+        + sems(data_devices - 1)
+        + sems(count - 1)
+        + sems(data_devices - 1) * 2
+        + sems(data_devices - 1)
+        + sems(count - 1),
+        compiler_params=pltpu.CompilerParams(
+            collective_id=3, has_side_effects=True, vmem_limit_bytes=58 * 2**20
+        ),
+    )(attended, gathered, dora, down, grad, grad_blocks)
 
 
 def on_device(
@@ -337,8 +507,10 @@
     def heads_of(rank):
         return lax.dynamic_slice_in_dim(image_rows, rank * head_width, head_width, 2)
 
+    late = seq_devices // 2
     image_blocks = [heads_of(seq_rank)] + [
-        shifted(heads_of((seq_rank + k) % seq_devices), k) for k in range(1, seq_devices)
+        None if k == late else shifted(heads_of((seq_rank + k) % seq_devices), k)
+        for k in range(1, seq_devices)
     ]
 
     direction = proj_weight.astype(f32) + jnp.dot(dora_a, dora_b, precision=lax.Precision.HIGHEST)
@@ -355,6 +527,8 @@
     hidden = (jax.nn.gelu(gate_proj, approximate=True) * upward).astype(bf16)
     ffn_part = jnp.dot(hidden, t5_out_weight, preferred_element_type=f32).astype(bf16)
     encoded, column_norm = feature_sum(ffn_part, own_tokens, own_final[None], squares)
+    late_heads, encoded = lax.optimization_barrier((heads_of((seq_rank + late) % seq_devices), encoded))
+    image_blocks[late] = shifted(late_heads, late)
     context_part = jnp.dot(encoded, context_columns, preferred_element_type=f32).astype(bf16)
     ratio = magnitude / column_norm[0]
     own_scaled = jnp.concatenate(
@@ -362,7 +536,7 @@
     )
     own_scaled, context_part = lax.optimization_barrier((own_scaled, context_part))
     gathered = lax.all_gather(own_scaled, "dp", axis=1, tiled=True)
-    scaled, scaled_up = gathered[: dora_a.shape[0]], gathered[dora_a.shape[0] :]
+    scaled_up = gathered[dora_a.shape[0] :]
     diffusion_length = jnp.sum(jnp.where(prompt_owner_sample == data_rank, lengths, 0))
     text_all = route(prompt_owner_sample, context_part, text_scale, text_shift)
 
@@ -370,39 +544,18 @@
 
     attended = attention(diffusion_length, text_key_gain, image_qk_gain, key_value, image_blocks)
 
-    rows = image_rows.shape[1]
-    up_rows = jnp.dot(attended, dora_a.astype(bf16), preferred_element_type=f32).astype(bf16)
     down = lax.dot_general(
         grad_out[0], scaled_up, (((1,), (1,)), ((), ())), preferred_element_type=f32
     ).astype(bf16)
-    down_rows = jnp.concatenate([down] + [shifted(down, k) for k in range(1, seq_devices)], 0)
-    total, up_total = 0.0, 0.0
-    for k in list(range(1, seq_devices)) + [0]:
-        block = attended[k * rows : (k + 1) * rows]
-        part = jnp.dot(block, scaled, preferred_element_type=f32).astype(bf16)
-        up_part = up_rows[k * rows : (k + 1) * rows]
-        if k:
-            part, up_part = shifted(part, seq_devices - k), shifted(up_part, seq_devices - k)
-        total, up_total = total + part.astype(f32), up_total + up_part.astype(f32)
-    image_out = total.astype(bf16)
-
-    grad_down = lax.dot_general(
-        attended, down_rows, (((0,), (0,)), ((), ())), preferred_element_type=f32
-    ).astype(bf16)
-    grad_up = lax.dot_general(
-        up_total.astype(bf16), grad_out[0], (((0,), (0,)), ((), ())), preferred_element_type=f32
-    )
-    grad_size = jnp.sum(grad_out[0].astype(f32) * total, 0, keepdims=True)
-    rank, data_devices = dora_b.shape[0], lax.axis_size("dp")
-    spare = jnp.zeros((15, grad_size.shape[1]), f32)
-    columns = jnp.concatenate([grad_up, grad_size, spare], 0).astype(bf16)
-    columns = columns.reshape(rank + 16, data_devices, -1).transpose(1, 0, 2)
-    column_sums, grad_a = gradient_sum(
-        columns, grad_down.reshape(data_devices, -1, rank)
-    )
-    grad_a = grad_a.reshape(-1, rank)
-    grad_b = column_sums[:rank] * ratio
-    grad_magnitude = column_sums[rank] / magnitude
+    data_devices = lax.axis_size("dp")
+    grad_blocks = grad_out[0].reshape(grad_out.shape[1], data_devices, -1).transpose(1, 0, 2)
+    image_out, sizes, column_sums, grad_a = finish_step(
+        attended, gathered, dora_a.astype(bf16), down, grad_out[0], grad_blocks
+    )
+    grad_a = grad_a.reshape(-1, dora_b.shape[0])
+    grad_b = column_sums * ratio
+    own_cols = magnitude.shape[0]
+    grad_magnitude = lax.dynamic_slice_in_dim(sizes[0], data_rank * own_cols, own_cols, 0) / magnitude
     return (image_out[None], grad_a, grad_b, grad_magnitude)
 
 

time: 309 us -> 291 us (0.942)
  Pallas kernels: 147 us -> 214 us
  waiting for transfers between devices: 54.3 us -> 0.75 us
  starting transfers between devices: 37.7 us -> 9.49 us
  matrix products: 43.2 us -> 31.8 us
  local copies, waits for them, and re-layouts: 8.3 us -> 14.8 us
    pallas_call x1, Pallas kernels: 15.6 us -> 87.1 us  [finish_step(): pl.pallas_call(finish_kernel, out_shape=[jax.ShapeDtypeStruct((rows, widt...]
    ppermute x12 -> x3, waiting for transfers between devices: 50.8 us -> 0.01 us  [shifted(): lax.ppermute(values, 'seq', [(i, (i + step) % seq_devices) for i in range...]
    ppermute x12 -> x3, starting transfers between devices: 37.5 us -> 9.37 us  [shifted(): lax.ppermute(values, 'seq', [(i, (i + step) % seq_devices) for i in range...]
    dot_general x7 -> x0, matrix products: 15 us -> none  [the longest x4 12.9 us: on_device(): part = jnp.dot(block, scaled, preferred_element_type=f32).astype(bf16)]
    pallas_call x1, Pallas kernels: 99.6 us -> 96 us  [route(): pl.pallas_call(route_kernel, out_shape=jax.ShapeDtypeStruct((text, width)...]
    unnamed x38 -> x22, local copies, waits for them, and re-layouts: 5.41 us -> 7.59 us
  transfers between devices with their start and end apart: 15 -> 6, of which waited for: 6 -> 0; matrix products, arithmetic and copies ran while one was open for 14% -> 15% of each run, Pallas kernels for 42% -> 44%
where the time goes in v3:
time: 291 us
  Pallas kernels  214 us (74%)
  matrix products  31.8 us (11%)
  local copies, waits for them, and re-layouts  14.8 us (5%)
  between operations  14 us (5%)
  starting transfers between devices  9.49 us (3%)
  other arithmetic  5.35 us (2%)
    pallas_call x1, Pallas kernels, route(): pl.pallas_call(route_kernel, out_shape=jax.ShapeDtypeStruct((text, width)...  96 us
    pallas_call x1, Pallas kernels, finish_step(): pl.pallas_call(finish_kernel, out_shape=[jax.ShapeDtypeStruct((rows, widt...  87.1 us
    pallas_call x1, Pallas kernels, feature_sum(): pl.pallas_call(feature_sum_kernel, out_shape=[jax.ShapeDtypeStruct((text,...  23.5 us
    dot_general x1, matrix products, on_device(): jnp.dot(hidden, t5_out_weight, preferred_element_type=f32).astype(bf16)  11 us
    ppermute x3, starting transfers between devices, shifted(): lax.ppermute(values, 'seq', [(i, (i + step) % seq_devices) for i in range...  9.37 us
    pallas_call x1, Pallas kernels, attention(): pl.pallas_call(functools.partial(attention_kernel, blocks), grid=(heads,)...  7.84 us
    unnamed x22, local copies, waits for them, and re-layouts  7.59 us
    dot_general x1, matrix products, on_device(): gate_proj = jnp.dot(normed, t5_in_weight[0], preferred_element_type=f32)  7.31 us
  transfers between devices with their start and end apart: 6, of which 0 were waited for; matrix products, arithmetic and copies ran while one was open for 15% of the time, Pallas kernels for 44%

profile of v3, /device:TPU:0, one launch (start us, length us, event | category | flops | bytes accessed | tf_op | source)
XLA Modules:
  0.0 290.6 jit_solution(8756335407062020703)
XLA Ops:
  7.9 2.4 copy.36
  10.5 0.8 copy-done.4
  11.4 2.3 multiply_reduce_fusion
  13.7 0.7 dynamic_slice.27
  14.4 1.5 fusion.12
  16.0 7.3 %fusion.24 = f32[128,1280]{1,0:T(8,128)} fusion(bf16[2,4096,1280]{2,1,0:T(8,128)(2,1)} %param.23, f32[4096]{0:T(1024)S(1)} %copy-done.8, f32[128]{0:T(128)S(1)} %add_rsqrt_fusion, bf16[1,256,4096]{2,1,0:T(8,128)(2,1)} %param.19), kind=kOutput, calls=%fused_computation.27 | convolution fusion | flops 1345585152 | bytes 12206592 | tf_op jit(solution)/shard_map/dot_general | solution.py:525
  23.3 11.0 %convolution_convert_fusion.part_ref = bf16[128,4096]{1,0:T(8,128)(2,1)S(1)} fusion(bf16[1280,4096]{1,0:T(8,128)(2,1)} %param.24, f32[128,1280]{1,0:T(8,128)} %fusion.24, bf16[2,4096,1280]{2,1,0:T(8,128)(2,1)} %param.23, f32[4096]{0:T(1024)S(1)} %copy-done.8, f32[128]{0:T(128)S(1)} %add_rsqrt_fusion, bf16[1,256,4096]{2,1,0:T(8,128)(2,1)} %param.19), kind=kOutput, calls=%fused_computation.6 | convolution fusion | flops 2687303680 | bytes 23740928 | tf_op jit(solution)/shard_map/dot_general | solution.py:528
  34.3 23.5 %shard_map.210 = (bf16[128,1024]{1,0:T(8,128)(2,1)S(1)}, f32[1,384]{1,0:T(1,128)S(1)}) custom-call(bf16[128,4096]{1,0:T(8,128)(2,1)S(1)} %convolution_convert_fusion.part_ref, bf16[128,1024]{1,0:T(8,128)(2,1)S(1)} %dynamic-slice_bitcast_fusion.4.tokens_ref, f32[1,1024]{1,0:T(1,128)S(1)} %bitcast.57, f32[1,384]{1,0:T(1,128)S(1)} %broadcast_in_dim.20.squares_ref), custom_call_target="tpu_custom_call" | custom-call | tf_op jit(solution)/shard_map/pallas_call | solution.py:156
  57.9 3.1 %dynamic-slice_bitcast_fusion = (bf16[3,128,768]{2,1,0:T(8,128)(2,1)}, bf16[3,128,768]{2,1,0:T(8,128)(2,1)}, bf16[3,128,768]{2,1,0:T(8,128)(2,1)}, bf16[3,128,768]{2,1,0:T(8,128)(2,1)}) fusion(bf16[1,128,3,3072]{3,1,2,0:T(8,128)(2,1)} %param.31, s32[]{:T(128)S(6)} %select_n.46, s32[]{:T(128)S(6)} %select_n.42, s32[]{:T(128)S(6)} %select_n.41, s32[]{:T(128)S(6)} %select_n.44), kind=kLoop, calls=%fused_computation.29 | loop fusion | bytes 4718608 | tf_op jit(solution)/shard_map/dynamic_slice | solution.py:508
  61.1 0.9 pad_maximum_fusion
  62.0 3.8 %convolution_convert_fusion.1.part_ref = bf16[128,3072]{1,0:T(8,128)(2,1)S(1)} fusion(bf16[128,1024]{1,0:T(8,128)(2,1)S(1)} %get-tuple-element.16, bf16[1024,3072]{1,0:T(8,128)(2,1)} %all-gather.4.cloned.1.call-done), kind=kOutput, calls=%fused_computation.7 | convolution fusion | flops 805699584 | bytes 7340032 | tf_op jit(solution)/shard_map/dot_general | solution.py:532
  65.9 5.2 %collective-permute-start.1 = (bf16[3,128,768]{2,1,0:T(8,128)(2,1)}, bf16[3,128,768]{2,1,0:T(8,128)(2,1)}, u32[]{:S(2)}, u32[]{:S(2)}) collective-permute-start(bf16[3,128,768]{2,1,0:T(8,128)(2,1)} %get-tuple-element.18), channel_id=1, source_target_pairs={{0,2},{1,3},{2,0},{3,1},{4,6},{5,7},{6,4},{7,5},{8,10},{9,11},{10,... | collective-permute-start | bytes 1769480 | tf_op jit(solution)/shard_map/ppermute | solution.py:498
  71.1 4.2 %collective-permute-start = (bf16[3,128,768]{2,1,0:T(8,128)(2,1)}, bf16[3,128,768]{2,1,0:T(8,128)(2,1)}, u32[]{:S(2)}, u32[]{:S(2)}) collective-permute-start(bf16[3,128,768]{2,1,0:T(8,128)(2,1)} %get-tuple-element.39), channel_id=1, source_target_pairs={{0,1},{1,2},{2,3},{3,0},{4,5},{5,6},{6,7},{7,4},{8,9},{9,10},{10,1... | collective-permute-start | bytes 1769480 | tf_op jit(solution)/shard_map/ppermute | solution.py:498
  75.7 1.2 copy.33
  76.9 0.8 copy.34.dora_ref
  78.4 96.0 %shard_map.211 = bf16[128,3072]{1,0:T(8,128)(2,1)S(1)} custom-call(s32[8]{0:T(128)S(1)} %copy-done.2, bf16[128,3072]{1,0:T(8,128)(2,1)S(1)} %convolution_convert_fusion.1.part_ref, f32[1,3072]{1,0:T(1,128)S(1)} %copy-done, f32[1,3072]{1,0:T(1,128)S(1)} %copy-done.1), custom_call_target="tpu_custom_call" | custom-call | tf_op jit(solution)/shard_map/pallas_call | solution.py:223
  174.4 6.0 %fusion.36.text_key_ref.text_value_ref = f32[128,1536]{1,0:T(8,128)} fusion(bf16[128,3072]{1,0:T(8,128)(2,1)S(1)} %shard_map.211, bf16[3072,1536]{1,0:T(8,128)(2,1)} %all-gather.6.cloned.1.call-done), kind=kOutput, calls=%fused_computation.44 | convolution fusion | flops 1207959552 | bytes 11010048 | tf_op jit(solution)/shard_map/dot_general | solution.py:543
  180.3 7.8 %shard_map.212.att_ref = bf16[512,768]{1,0:T(8,128)(2,1)} custom-call(s32[1]{0:T(128)} %bitcast.length_ref, f32[1,128]{1,0:T(1,128)} %bitcast.66, f32[2,128]{1,0:T(2,128)} %image_gain_ref.1, f32[128,1536]{1,0:T(8,128)} %fusion.36.text_key_ref.text_value_ref, f32[128,1536]{1,0:T(8,128)} %fusion.36.text_key_ref.text_value_ref, ...), custom_call_target="tpu_custom_call" | custom-call | flops 1006632960 | bytes 3145728 | tf_op jit(solution)/shard_map/pallas_call | solution.py:55
  188.2 1.4 convolution_convert_fusion.2
  189.6 0.7 copy.31
  190.3 87.1 %shard_map.213 = (bf16[128,3072]{1,0:T(8,128)(2,1)}, f32[1,3072]{1,0:T(1,128)}, f32[64,384]{1,0:T(8,128)}, f32[8,96,64]{2,1,0:T(8,128)}) custom-call(bf16[512,768]{1,0:T(8,128)(2,1)} %shard_map.212.att_ref, bf16[832,3072]{1,0:T(8,128)(2,1)} %all-gather.8.cloned.1.call-done.weight_ref, bf16[768,64]{1,0:T(8,128)(2,1)} %copy.34.dora_ref, ...), custom_call_target="tpu_custom_call" | custom-call | tf_op jit(solution)/shard_map/pallas_call | solution.py:427
  277.4 1.5 broadcast_multiply_fusion
  278.9 1.8 copy.35
  282.1 2.1 copy.38
  (44 shorter events, 3.4 us)
Async XLA Ops:
  7.2 54.8 %all-gather.4.cloned.1.call-start = ((), (), s32[]{:S(2)}) async-start(), calls=%async_computation | async-start | bytes 7077888 | tf_op jit(solution)/shard_map/all_gather | solution.py:501
  7.9 166.5 %all-gather.6.cloned.1.call-start = ((), (), s32[]{:S(2)}) async-start(), calls=%async_computation.1 | async-start | bytes 10616832 | tf_op jit(solution)/shard_map/all_gather | solution.py:502
  10.4 0.9 copy-start.4
  10.4 1.0 copy-start.5
  10.4 177.8 %all-gather.8.cloned.1.call-start = ((), (), s32[]{:S(2)}) async-start(), calls=%async_computation.2 | async-start | bytes 5750784 | tf_op jit(solution)/shard_map/all_gather | solution.py:538
  10.5 3.9 %slice-start = ((bf16[1,256,4096]{2,1,0:T(8,128)(2,1)}), bf16[1,128,4096]{2,1,0:T(8,128)(2,1)S(1)}, s32[]{:S(2)}) async-start(bf16[1,256,4096]{2,1,0:T(8,128)(2,1)} %param.19), calls=%async_computation.3 | async-start | bytes 2097152 | tf_op jit(solution)/shard_map/slice | solution.py:519
  11.4 4.6 %copy-start.8 = (f32[4096]{0:T(1024)S(1)}, f32[4096]{0:T(1024)}, u32[]{:S(2)}) copy-start(f32[4096]{0:T(1024)} %param.22) | copy-start | bytes 49156
  57.9 3.1 %copy-start.6 = (f32[384]{0:T(512)S(1)}, f32[384]{0:T(512)}, u32[]{:S(2)}) copy-start(f32[384]{0:T(512)} %param.36) | copy-start | bytes 4612
  62.0 13.3 %copy-start.3 = (bf16[1,128,3072]{2,1,0:T(8,128)(2,1)S(1)}, bf16[1,128,3072]{2,1,0:T(8,128)(2,1)}, u32[]{:S(2)}) copy-start(bf16[1,128,3072]{2,1,0:T(8,128)(2,1)} %param.37) | copy-start | bytes 2359300
  65.8 11.9 %copy-start.2 = (s32[8]{0:T(128)S(1)}, s32[8]{0:T(128)}, u32[]{:S(2)}) copy-start(s32[8]{0:T(128)} %owner_ref.1) | copy-start | bytes 100
  65.9 11.9 %copy-start.7 = (s32[8]{0:T(128)S(1)}, s32[8]{0:T(128)}, u32[]{:S(2)}) copy-start(s32[8]{0:T(128)} %param.20) | copy-start | bytes 100
  65.9 12.5 %copy-start = (f32[1,3072]{1,0:T(1,128)S(1)}, f32[1,3072]{1,0:T(1,128)}, u32[]{:S(2)}) copy-start(f32[1,3072]{1,0:T(1,128)} %scale_ref.1) | copy-start | bytes 36868
  65.9 12.5 %copy-start.1 = (f32[1,3072]{1,0:T(1,128)S(1)}, f32[1,3072]{1,0:T(1,128)}, u32[]{:S(2)}) copy-start(f32[1,3072]{1,0:T(1,128)} %shift_ref.1) | copy-start | bytes 36868
  65.9 114.4 %collective-permute-start.1 = (bf16[3,128,768]{2,1,0:T(8,128)(2,1)}, bf16[3,128,768]{2,1,0:T(8,128)(2,1)}, u32[]{:S(2)}, u32[]{:S(2)}) collective-permute-start(bf16[3,128,768]{2,1,0:T(8,128)(2,1)} %get-tuple-element.18), channel_id=1, source_target_pairs={{0,2},{1,3},{2,0},{3,1},{4,6},{5,7},{6,4},{7,5},{8,10},{9,11},{10,... | collective-permute-start | bytes 1769480 | tf_op jit(solution)/shard_map/ppermute | solution.py:498
  71.1 109.3 %collective-permute-start = (bf16[3,128,768]{2,1,0:T(8,128)(2,1)}, bf16[3,128,768]{2,1,0:T(8,128)(2,1)}, u32[]{:S(2)}, u32[]{:S(2)}) collective-permute-start(bf16[3,128,768]{2,1,0:T(8,128)(2,1)} %get-tuple-element.39), channel_id=1, source_target_pairs={{0,1},{1,2},{2,3},{3,0},{4,5},{5,6},{6,7},{7,4},{8,9},{9,10},{10,1... | collective-permute-start | bytes 1769480 | tf_op jit(solution)/shard_map/ppermute | solution.py:498
  75.3 105.1 %collective-permute-start.2 = (bf16[3,128,768]{2,1,0:T(8,128)(2,1)}, bf16[3,128,768]{2,1,0:T(8,128)(2,1)}, u32[]{:S(2)}, u32[]{:S(2)}) collective-permute-start(bf16[3,128,768]{2,1,0:T(8,128)(2,1)} %get-tuple-element.36), channel_id=1, source_target_pairs={{0,3},{1,0},{2,1},{3,2},{4,7},{5,4},{6,5},{7,6},{8,11},{9,8},{10,9... | collective-permute-start | bytes 1769480 | tf_op jit(solution)/shard_map/ppermute | solution.py:498
Sparse Core Ops, SparseCore 0:
  9.8 49.2 all-gather.3
  61.1 58.6 all-gather.5
  121.7 50.7 all-gather.7
